TPU v7x, 512 devices: a whole 4x8x8 slice. The times are simulated.
512 devices in a mesh: shell: 8 (over z), row: 4 (over x_hi, core), col: 16 (over x_lo, y).
Axes of the slice: x: 4 (x_hi: 2, x_lo: 2; x = x_hi * 2 + x_lo), y: 8, z: 8, core: 2. Of those that a mesh axis runs over, the one named last changes fastest.
Arguments:
- left_basis: bfloat16 [2, 4096, 6144], P(None, 'row', 'shell'), may hold values from -6 to 6
- right_basis: bfloat16 [2, 6144, 8192], P(None, 'shell', 'col'), may hold values from -0.078125 to 0.078125
- point_weight: float32 [6144], P('shell'), may hold values from 0.3 to 3
- shell_index: int32 [6144], P('shell'), may hold values from 0 to 11
- green_table: float32 [12, 2], replicated, may hold values from -4 to 4
- pivot_rows: int32 [512], replicated, may hold values from 0 to 4095, as said below
- diag_inverse: bfloat16 [2, 512, 512], replicated, may hold values from -0.005859375 to 0.005859375
Outputs:
- factored: float32 [2, 4, 8, 128, 8192], P(None, 'row', 'shell', None, 'col')
Inputs may be any that keep to these rules, and one draw needn't show every extreme that they name: `pivot_rows`: 512 distinct matrix rows.
All inputs are finite; a program needn't handle non-finite values.
Results may differ from a plain program's by a relative error of at most 0.0056.
Values may be sent and summed in bfloat16 or wider, within the bound.
No kernel may reach another device: no remote copies, remote signals or barrier semaphores. Data moves between devices by JAX's collectives and lax.ppermute only.
A program may use at most 128 MiB of HBM per device.

v0:
```python
import jax
import jax.numpy as jnp
from jax import lax
from jax.sharding import PartitionSpec as P


def broadcast(block, axis, source):
    block = jnp.where(lax.axis_index(axis) == source, block, jnp.zeros_like(block))
    return lax.psum(block, axis)


def complex_block(real_part, imag_part):
    upper_half = jnp.concatenate([real_part, imag_part], axis=1)
    lower_half = jnp.concatenate([-imag_part, real_part], axis=1)
    return jnp.concatenate([upper_half, lower_half], axis=0)


def weigh_points(right_basis, point_weight, shell_index, green_table):
    shells_count = green_table.shape[0]
    matches = shell_index[:, None] == jnp.arange(shells_count, dtype=jnp.int32)[None, :]
    green_real = jnp.sum(jnp.where(matches, green_table[None, :, 0], 0.0), axis=1)
    green_imag = jnp.sum(jnp.where(matches, green_table[None, :, 1], 0.0), axis=1)
    weight_real = point_weight * green_real
    weight_imag = point_weight * green_imag
    basis_real = right_basis[0].astype(jnp.float32)
    basis_imag = right_basis[1].astype(jnp.float32)
    weighted_real = (weight_real[:, None] * basis_real - weight_imag[:, None] * basis_imag).astype(
        jnp.bfloat16
    )
    weighted_imag = (weight_real[:, None] * basis_imag + weight_imag[:, None] * basis_real).astype(
        jnp.bfloat16
    )
    return (weighted_real, weighted_imag)


def reduce_tiles(term_rows, owned_rows):
    return lax.psum_scatter(
        term_rows(jnp.int32(0), owned_rows * lax.axis_size("shell")),
        "shell",
        scatter_dimension=0,
        tiled=True,
    )


def pick_rows(matrix_rows, pivot_rows, row_base):
    held_rows = matrix_rows.shape[0]
    local_index = pivot_rows - row_base
    inside = (local_index >= 0) & (local_index < held_rows)
    picked = jnp.take(matrix_rows, jnp.clip(local_index, 0, held_rows - 1), axis=0)
    return jnp.where(inside[:, None], picked, 0.0)


def select_pivots(coupling, pivot_rows, row_base):
    picked = pick_rows(coupling, pivot_rows, row_base).astype(jnp.bfloat16)
    return lax.psum(picked, ("shell", "row")).astype(jnp.float32).astype(jnp.bfloat16)


def body(left_basis, right_basis, point_weight, shell_index, green_table, pivot_rows, diag_inverse):
    shells = lax.axis_size("shell")
    owned_rows = left_basis.shape[1] // shells
    panel_width = right_basis.shape[2]
    weighted_real, weighted_imag = weigh_points(right_basis, point_weight, shell_index, green_table)
    grid_row = lax.axis_index("row")
    shell_rank = lax.axis_index("shell")
    row_base = (grid_row * shells + shell_rank) * owned_rows
    left_stack = jnp.concatenate([left_basis[0], left_basis[1]], axis=1)
    right_stack = complex_block(weighted_real, weighted_imag)

    def from_bases(first_row, row_count):
        return jnp.dot(left_stack, right_stack, preferred_element_type=jnp.float32)

    coupling = reduce_tiles(from_bases, owned_rows)
    pivot_sum = select_pivots(coupling, pivot_rows, row_base)
    panel_real = coupling[:, :panel_width]
    panel_imag = coupling[:, panel_width:]
    inverse_real = diag_inverse[0].astype(jnp.float32)
    inverse_imag = diag_inverse[1].astype(jnp.float32)
    highest = lax.Precision.HIGHEST
    mult_real = (
        jnp.dot(panel_real, inverse_real, precision=highest, preferred_element_type=jnp.float32)
        - jnp.dot(panel_imag, inverse_imag, precision=highest, preferred_element_type=jnp.float32)
    ).astype(jnp.bfloat16)
    mult_imag = (
        jnp.dot(panel_real, inverse_imag, precision=highest, preferred_element_type=jnp.float32)
        + jnp.dot(panel_imag, inverse_real, precision=highest, preferred_element_type=jnp.float32)
    ).astype(jnp.bfloat16)
    multipliers = jnp.concatenate([mult_real, mult_imag], axis=1)
    multipliers = broadcast(multipliers, "col", 0)
    pivot_block = complex_block(pivot_sum[:, :panel_width], pivot_sum[:, panel_width:])
    update = jnp.dot(multipliers, pivot_block, preferred_element_type=jnp.float32)
    updated = coupling - update
    return jnp.stack([updated[:, :panel_width], updated[:, panel_width:]]).reshape(
        2, 1, 1, owned_rows, panel_width
    )


def solution(mesh):
    return jax.shard_map(
        body,
        mesh=mesh,
        in_specs=(
            P(None, "row", "shell"),
            P(None, "shell", "col"),
            P("shell"),
            P("shell"),
            P(),
            P(),
            P(),
        ),
        out_specs=P(None, "row", "shell", None, "col"),
        check_vma=False,
    )
```

profile of v0, /device:TPU:4, one launch (start us, length us, event | category | flops | bytes accessed | tf_op | source)
XLA Modules:
  0.0 509.2 jit_solution(4400206457405959289)
XLA Ops:
  6.5 0.0 reduce-scatter.2.cloned.1.call-start
  6.5 0.8 slice_bitcast_fusion.4
  7.4 0.8 select_reduce_fusion.1
  8.1 0.7 fusion.44
  8.8 1.9 fusion.42
  10.8 0.0 copy-done.1
  10.8 0.4 fusion.18
  11.2 0.0 copy-done.3
  11.2 0.2 slice_bitcast_fusion.1
  11.4 5.3 %fusion = f32[1024,1024]{1,0:T(8,128)} fusion(bf16[1024,768]{1,0:T(8,128)(2,1)S(1)} %get-tuple-element.12, bf16[1024,768]{1,0:T(8,128)(2,1)S(1)} %get-tuple-element.11, bf16[768,512]{1,0:T(8,128)(2,1)S(1)} %fusion.18, bf16[768,512]{1,0:T(8,128)(2,1)S(1)} %get-tuple-element.9, bf16[768,512]{1,0:T(8,128)(2,1)S(1)} %get-tuple-element.10), kind=kOutput, calls=%fused_computation.1 | convolution fusion | flops 3240099840 | bytes 9699328 | tf_op jit(solution)/shard_map/dot_general | solution.py:70
  16.7 0.0 reduce-scatter.2.cloned.1.call-update
  16.8 0.0 all-reduce.5.cloned.1.call-start
  16.8 0.6 copy-done.5
  17.4 62.8 %reduce-scatter.2.cloned.1.call-done = f32[128,1024]{1,0:T(8,128)} async-done(((f32[1024,1024]{1,0:T(8,128)}), f32[128,1024]{1,0:T(8,128)}) %reduce-scatter.2.cloned.1.call-update) | async-done | bytes 524304 | tf_op jit(solution)/shard_map/reduce_scatter | solution.py:37
  80.3 3.8 gather_fusion
  84.0 0.0 copy-start
  84.0 0.0 copy-start.2
  84.1 1.4 select_convert_fusion
  85.4 0.0 all-reduce.5.cloned.1.call-update
  85.4 0.0 all-reduce.3.cloned.1.call-start
  85.5 0.2 copy-done.2
  85.7 0.4 fusion.30
  86.1 0.4 fusion.26
  86.4 0.4 fusion.24
  86.8 0.4 fusion.25
  87.2 0.8 maximum_select_fusion
  88.0 0.0 all-reduce.3.cloned.1.call-update
  88.0 267.2 %all-reduce.5.cloned.1.call-done = bf16[512,1024]{1,0:T(8,128)(2,1)} async-done(((bf16[512,1024]{1,0:T(8,128)(2,1)}), bf16[512,1024]{1,0:T(8,128)(2,1)}) %all-reduce.5.cloned.1.call-update) | async-done | bytes 1048592 | tf_op jit(solution)/shard_map/psum | solution.py:55
  355.2 1.4 slice_negate_fusion
  356.6 143.8 %all-reduce.3.cloned.1.call-done = bf16[128,1024]{1,0:T(8,128)(2,1)} async-done(((bf16[128,1024]{1,0:T(8,128)(2,1)}), bf16[128,1024]{1,0:T(8,128)(2,1)}) %all-reduce.3.cloned.1.call-update) | async-done | bytes 262160 | tf_op jit(solution)/shard_map/psum | solution.py:9
  500.4 1.4 fusion.21
  501.8 0.8 maximum_bitcast_fusion
  (9 shorter events, 0.1 us)
Async XLA Ops:
  6.5 4.2 copy-start.1
  6.5 73.7 %reduce-scatter.2.cloned.1.call-start = ((), (), s32[]{:S(2)}) async-start(), calls=%async_computation.1 | async-start | bytes 4718592 | tf_op jit(solution)/shard_map/reduce_scatter | solution.py:37
  8.8 2.4 copy-start.3
  16.7 0.7 copy-start.5
  16.8 338.4 %all-reduce.5.cloned.1.call-start = ((), (), s32[]{:S(2)}) async-start(), calls=%async_computation.3 | async-start | bytes 2097152 | tf_op jit(solution)/shard_map/psum | solution.py:55
  84.0 1.5 copy-start
  84.0 1.6 copy-start.2
  85.4 414.9 %all-reduce.3.cloned.1.call-start = ((), (), s32[]{:S(2)}) async-start(), calls=%async_computation.2 | async-start | bytes 524288 | tf_op jit(solution)/shard_map/psum | solution.py:9
  355.2 145.2 %copy-start.4 = (bf16[512,1024]{1,0:T(8,128)(2,1)S(1)}, bf16[512,1024]{1,0:T(8,128)(2,1)}, u32[]{:S(2)}) copy-start(bf16[512,1024]{1,0:T(8,128)(2,1)} %all-reduce.5.cloned.1.call-done) | copy-start | bytes 3145732
Sparse Core Ops, SparseCore 0:
  16.9 63.3 reduce-scatter.1
  85.6 269.6 all-reduce.4
  358.4 141.9 all-reduce.2
where the time goes:
time: 509 us
  waiting for transfers between devices  474 us (93%)
  between operations  13.2 us (3%)
  matrix products  8.23 us (2%)
  other arithmetic  8.1 us (2%)
  local copies, waits for them, and re-layouts  5.65 us (1%)
    psum x1, waiting for transfers between devices, select_pivots(): lax.psum(picked, ('shell', 'row')).astype(jnp.float32).astype(jnp.bfloat16)  267 us
    psum x1, waiting for transfers between devices, broadcast(): return lax.psum(block, axis)  144 us
    reduce_scatter x1, waiting for transfers between devices, reduce_tiles(): lax.psum_scatter(term_rows(jnp.int32(0), owned_rows * lax.axis_size('shel...  62.8 us
  transfers between devices with their start and end apart: 3, of which 3 were waited for; matrix products, arithmetic and copies ran while one was open for 1% of the time, Pallas kernels for 0%

commit v1 on v0

v1 whole, which is shorter than its diff:
```python
import jax
import jax.numpy as jnp
from jax import lax
from jax.sharding import PartitionSpec as P

BF16 = jnp.bfloat16
F32 = jnp.float32
GRID = ("shell", "row")


def complex_block(real_part, imag_part):
    upper_half = jnp.concatenate([real_part, imag_part], axis=1)
    lower_half = jnp.concatenate([-imag_part, real_part], axis=1)
    return jnp.concatenate([upper_half, lower_half], axis=0)


def weigh_points(right_basis, point_weight, shell_index, green_table):
    shells_count = green_table.shape[0]
    matches = shell_index[:, None] == jnp.arange(shells_count, dtype=jnp.int32)[None, :]
    green_real = jnp.sum(jnp.where(matches, green_table[None, :, 0], 0.0), axis=1)
    green_imag = jnp.sum(jnp.where(matches, green_table[None, :, 1], 0.0), axis=1)
    weight_real = point_weight * green_real
    weight_imag = point_weight * green_imag
    basis_real = right_basis[0].astype(F32)
    basis_imag = right_basis[1].astype(F32)
    weighted_real = (weight_real[:, None] * basis_real - weight_imag[:, None] * basis_imag).astype(BF16)
    weighted_imag = (weight_real[:, None] * basis_imag + weight_imag[:, None] * basis_real).astype(BF16)
    return (weighted_real, weighted_imag)


def exchange(blocks, axes):
    return lax.all_to_all(blocks, axes, 0, 0, tiled=False)


def gather_blocks(block, axes, count):
    return exchange(jnp.broadcast_to(block[None], (count,) + block.shape), axes)


def body(left_basis, right_basis, point_weight, shell_index, green_table, pivot_rows, diag_inverse):
    shells = lax.axis_size("shell")
    grid_rows = lax.axis_size("row")
    columns = lax.axis_size("col")
    holders = shells * grid_rows
    tile_rows = left_basis.shape[1]
    owned_rows = tile_rows // shells
    width = right_basis.shape[2]
    pivots_count = pivot_rows.shape[0]
    weighted_real, weighted_imag = weigh_points(right_basis, point_weight, shell_index, green_table)
    left_stack = jnp.concatenate([left_basis[0], left_basis[1]], axis=1)
    right_stack = complex_block(weighted_real, weighted_imag)
    terms = jnp.dot(left_stack, right_stack, preferred_element_type=F32).astype(BF16)

    coupling = lax.psum_scatter(terms, "shell", scatter_dimension=0, tiled=True).astype(F32)

    tile_index = lax.broadcasted_iota(jnp.int32, (pivots_count, tile_rows), 1) + lax.axis_index("row") * tile_rows
    chosen = (pivot_rows[:, None] == tile_index).astype(BF16)
    picked = jnp.dot(chosen, terms, preferred_element_type=F32).astype(BF16)
    shares = exchange(picked.reshape(holders, pivots_count // holders, 2 * width), GRID)
    pivot_share = jnp.sum(shares.astype(F32), axis=0).astype(BF16)
    pivots = gather_blocks(pivot_share, GRID, holders).reshape(pivots_count, 2 * width)

    panel_real = coupling[:, :width]
    panel_imag = coupling[:, width:]
    inverse_real = diag_inverse[0].astype(F32)
    inverse_imag = diag_inverse[1].astype(F32)
    highest = lax.Precision.HIGHEST
    mult_real = (
        jnp.dot(panel_real, inverse_real, precision=highest, preferred_element_type=F32)
        - jnp.dot(panel_imag, inverse_imag, precision=highest, preferred_element_type=F32)
    ).astype(BF16)
    mult_imag = (
        jnp.dot(panel_real, inverse_imag, precision=highest, preferred_element_type=F32)
        + jnp.dot(panel_imag, inverse_real, precision=highest, preferred_element_type=F32)
    ).astype(BF16)
    multipliers = jnp.concatenate([mult_real, mult_imag], axis=1)
    spread = exchange(multipliers.reshape(columns, owned_rows // columns, 2 * width), "col")[0]
    multipliers = gather_blocks(spread, "col", columns).reshape(owned_rows, 2 * width)

    pivot_block = complex_block(pivots[:, :width], pivots[:, width:])
    updated = coupling - jnp.dot(multipliers, pivot_block, preferred_element_type=F32)
    return jnp.stack([updated[:, :width], updated[:, width:]]).reshape(2, 1, 1, owned_rows, width)


def solution(mesh):
    return jax.shard_map(
        body,
        mesh=mesh,
        in_specs=(
            P(None, "row", "shell"),
            P(None, "shell", "col"),
            P("shell"),
            P("shell"),
            P(),
            P(),
            P(),
        ),
        out_specs=P(None, "row", "shell", None, "col"),
        check_vma=False,
    )
```

time: 509 us -> 168 us (0.33)
  the two profiles are of different devices: /device:TPU:4 before, /device:TPU:14 now
where the time goes in v1:
time: 168 us; the launch traced here: 167 us
  waiting for transfers between devices  96.6 us (58%)
  starting transfers between devices  35.8 us (21%)
  between operations  13.5 us (8%)
  matrix products  11.2 us (7%)
  other arithmetic  5.58 us (3%)
  local copies, waits for them, and re-layouts  4.47 us (3%)
    reduce_scatter x1, waiting for transfers between devices, body(): lax.psum_scatter(terms, 'shell', scatter_dimension=0, tiled=True)  49.6 us
    all_to_all x4, waiting for transfers between devices, exchange(): return lax.all_to_all(blocks, axes, 0, 0, tiled=False)  46.9 us
    all_to_all x4, starting transfers between devices, exchange(): return lax.all_to_all(blocks, axes, 0, 0, tiled=False)  35.8 us
    dot_general x1, matrix products, body(): jnp.dot(left_stack, right_stack, preferred_element_type=F32).astype(BF16)  4.74 us
  transfers between devices with their start and end apart: 5, of which 4 were waited for; matrix products, arithmetic and copies ran while one was open for 4% of the time, Pallas kernels for 0%

profile of v1, /device:TPU:14, one launch (start us, length us, event | category | flops | bytes accessed | tf_op | source)
XLA Modules:
  0.0 167.1 jit_solution(3308490682110224936)
XLA Ops:
  6.5 0.8 slice_bitcast_fusion.5
  7.4 0.8 select_reduce_fusion.1
  8.1 0.7 fusion.57
  8.8 1.9 %fusion.55 = (bf16[768,512]{1,0:T(8,128)(2,1)S(1)}, bf16[768,512]{1,0:T(8,128)(2,1)S(1)}) fusion(bf16[2,768,512]{2,1,0:T(8,128)(2,1)} %param.8, f32[768]{0:T(1024)S(1)} %get-tuple-element.16, f32[768]{0:T(1024)S(1)} %get-tuple-element.15), kind=kLoop, calls=%fused_computation.67 | loop fusion | flops 2752512 | bytes 3151872 | tf_op jit(solution)/shard_map/neg | solution.py:13
  10.8 0.4 fusion.25
  11.2 0.0 copy-done.2
  11.2 0.2 slice_bitcast_fusion.1
  11.4 4.7 %fusion.19 = bf16[1024,1024]{1,0:T(8,128)(2,1)} fusion(bf16[768,512]{1,0:T(8,128)(2,1)S(1)} %fusion.25, bf16[768,512]{1,0:T(8,128)(2,1)S(1)} %get-tuple-element.7, bf16[768,512]{1,0:T(8,128)(2,1)S(1)} %get-tuple-element.8, bf16[1024,768]{1,0:T(8,128)(2,1)S(1)} %get-tuple-element.10, bf16[1024,768]{1,0:T(8,128)(2,1)S(1)} %get-tuple-element.9), kind=kOutput, calls=%fused_computation.23 | convolution fusion | flops 3241148416 | bytes 7602176 | tf_op jit(solution)/shard_map/dot_general | solution.py:51
  16.1 0.0 reduce-scatter.2.cloned.1.call-update
  16.2 1.5 copy-done.3
  17.7 0.0 copy-done.5
  17.7 2.3 %fusion.28 = bf16[512,1024]{1,0:T(8,128)(2,1)} fusion(bf16[1024,1024]{1,0:T(8,128)(2,1)S(1)} %copy-done.3, s32[1024]{0:T(1024)S(1)} %iota_add_fusion, s32[512]{0:T(512)S(1)} %copy-done.5), kind=kOutput, calls=%fused_computation.30 | convolution fusion | flops 1074790400 | bytes 3151872 | tf_op jit(solution)/shard_map/dot_general | solution.py:57
  20.0 13.6 %all-to-all-start.2 = ((bf16[32,16,1024]{2,1,0:T(8,128)(2,1)}), bf16[32,16,1024]{2,1,0:T(8,128)(2,1)S(1)}, u32[]{:S(2)}, u32[]{:S(2)}) async-start(bf16[32,16,1024]{2,1,0:T(8,128)(2,1)} %bitcast.13), calls=%async_computation.3 | async-start | bytes 2097152 | tf_op jit(solution)/shard_map/all_to_all | solution.py:32
  33.6 49.6 %reduce-scatter.2.cloned.1.call-done = bf16[128,1024]{1,0:T(8,128)(2,1)} async-done(((bf16[1024,1024]{1,0:T(8,128)(2,1)}), bf16[128,1024]{1,0:T(8,128)(2,1)}) %reduce-scatter.2.cloned.1.call-update) | async-done | bytes 262160 | tf_op jit(solution)/shard_map/reduce_scatter | solution.py:53
  83.2 1.2 fusion.42
  84.4 1.1 fusion.38
  85.6 1.1 fusion.34
  86.7 0.2 fusion.35
  86.9 0.7 maximum_bitcast_fusion.1
  87.7 0.0 all-to-all-done.2
  87.7 8.6 %all-to-all-start = ((bf16[16,8,1024]{2,1,0:T(8,128)(2,1)}), bf16[16,8,1024]{2,1,0:T(8,128)(2,1)S(1)}, u32[]{:S(2)}, u32[]{:S(2)}) async-start(bf16[16,8,1024]{2,1,0:T(8,128)(2,1)} %maximum_bitcast_fusion.1), calls=%async_computation.1 | async-start | bytes 524288 | tf_op jit(solution)/shard_map/all_to_all | solution.py:32
  96.2 0.2 reduce_sum.32
  96.4 8.5 %all-to-all-done = bf16[16,8,1024]{2,1,0:T(8,128)(2,1)S(1)} async-done(((bf16[16,8,1024]{2,1,0:T(8,128)(2,1)}), bf16[16,8,1024]{2,1,0:T(8,128)(2,1)S(1)}, u32[]{:S(2)}, u32[]{:S(2)}) %all-to-all-start) | async-done | bytes 262176 | tf_op jit(solution)/shard_map/all_to_all | solution.py:32
  104.9 1.1 broadcast_in_dim.49
  106.0 9.1 %all-to-all-start.3 = ((bf16[32,16,1024]{2,1,0:T(8,128)(2,1)}), bf16[32,16,1024]{2,1,0:T(8,128)(2,1)S(1)}, u32[]{:S(2)}, u32[]{:S(2)}) async-start(bf16[32,16,1024]{2,1,0:T(8,128)(2,1)} %broadcast_in_dim.49), calls=%async_computation.4 | async-start | bytes 2097152 | tf_op jit(solution)/shard_map/all_to_all | solution.py:32
  115.2 28.9 %all-to-all-done.3 = bf16[32,16,1024]{2,1,0:T(8,128)(2,1)S(1)} async-done(((bf16[32,16,1024]{2,1,0:T(8,128)(2,1)}), bf16[32,16,1024]{2,1,0:T(8,128)(2,1)S(1)}, u32[]{:S(2)}, u32[]{:S(2)}) %all-to-all-start.3) | async-done | bytes 1048608 | tf_op jit(solution)/shard_map/all_to_all | solution.py:32
  144.1 0.7 broadcast_in_dim.48
  144.8 4.5 %all-to-all-start.1 = ((bf16[16,8,1024]{2,1,0:T(8,128)(2,1)}), bf16[16,8,1024]{2,1,0:T(8,128)(2,1)S(1)}, u32[]{:S(2)}, u32[]{:S(2)}) async-start(bf16[16,8,1024]{2,1,0:T(8,128)(2,1)} %broadcast_in_dim.48), calls=%async_computation.2 | async-start | bytes 524288 | tf_op jit(solution)/shard_map/all_to_all | solution.py:32
  149.3 0.1 slice_negate_fusion
  149.4 9.5 %all-to-all-done.1 = bf16[16,8,1024]{2,1,0:T(8,128)(2,1)S(1)} async-done(((bf16[16,8,1024]{2,1,0:T(8,128)(2,1)}), bf16[16,8,1024]{2,1,0:T(8,128)(2,1)S(1)}, u32[]{:S(2)}, u32[]{:S(2)}) %all-to-all-start.1) | async-done | bytes 262176 | tf_op jit(solution)/shard_map/all_to_all | solution.py:32
  158.9 0.4 fusion.31
  159.4 0.8 maximum_bitcast_fusion
  (13 shorter events, 0.1 us)
Async XLA Ops:
  6.5 4.2 %copy-start = (bf16[2,768,512]{2,1,0:T(8,128)(2,1)S(1)}, bf16[2,768,512]{2,1,0:T(8,128)(2,1)}, u32[]{:S(2)}) copy-start(bf16[2,768,512]{2,1,0:T(8,128)(2,1)} %param.8) | copy-start | bytes 4718596
  6.5 76.7 %reduce-scatter.2.cloned.1.call-start = ((), (), s32[]{:S(2)}) async-start(), calls=%async_computation.5 | async-start | bytes 2359296 | tf_op jit(solution)/shard_map/reduce_scatter | solution.py:53
  8.8 2.4 %copy-start.2 = (bf16[2,1024,768]{2,1,0:T(8,128)(2,1)S(1)}, bf16[2,1024,768]{2,1,0:T(8,128)(2,1)}, u32[]{:S(2)}) copy-start(bf16[2,1024,768]{2,1,0:T(8,128)(2,1)} %param.7) | copy-start | bytes 9437188
  16.1 1.6 copy-start.3
  16.1 1.6 copy-start.5
  20.0 63.2 %copy-start.1 = (bf16[2,512,512]{2,1,0:T(8,128)(2,1)S(1)}, bf16[2,512,512]{2,1,0:T(8,128)(2,1)}, u32[]{:S(2)}) copy-start(bf16[2,512,512]{2,1,0:T(8,128)(2,1)} %param.13) | copy-start | bytes 3145732
  20.0 67.7 %all-to-all-start.2 = ((bf16[32,16,1024]{2,1,0:T(8,128)(2,1)}), bf16[32,16,1024]{2,1,0:T(8,128)(2,1)S(1)}, u32[]{:S(2)}, u32[]{:S(2)}) async-start(bf16[32,16,1024]{2,1,0:T(8,128)(2,1)} %bitcast.13), calls=%async_computation.3 | async-start | bytes 2097152 | tf_op jit(solution)/shard_map/all_to_all | solution.py:32
  83.2 3.5 %copy-start.4 = (bf16[128,1024]{1,0:T(8,128)(2,1)S(1)}, bf16[128,1024]{1,0:T(8,128)(2,1)}, u32[]{:S(2)}) copy-start(bf16[128,1024]{1,0:T(8,128)(2,1)} %reduce-scatter.2.cloned.1.call-done) | copy-start | bytes 786436
  87.7 17.2 %all-to-all-start = ((bf16[16,8,1024]{2,1,0:T(8,128)(2,1)}), bf16[16,8,1024]{2,1,0:T(8,128)(2,1)S(1)}, u32[]{:S(2)}, u32[]{:S(2)}) async-start(bf16[16,8,1024]{2,1,0:T(8,128)(2,1)} %maximum_bitcast_fusion.1), calls=%async_computation.1 | async-start | bytes 524288 | tf_op jit(solution)/shard_map/all_to_all | solution.py:32
  106.0 38.1 %all-to-all-start.3 = ((bf16[32,16,1024]{2,1,0:T(8,128)(2,1)}), bf16[32,16,1024]{2,1,0:T(8,128)(2,1)S(1)}, u32[]{:S(2)}, u32[]{:S(2)}) async-start(bf16[32,16,1024]{2,1,0:T(8,128)(2,1)} %broadcast_in_dim.49), calls=%async_computation.4 | async-start | bytes 2097152 | tf_op jit(solution)/shard_map/all_to_all | solution.py:32
  144.8 14.1 %all-to-all-start.1 = ((bf16[16,8,1024]{2,1,0:T(8,128)(2,1)}), bf16[16,8,1024]{2,1,0:T(8,128)(2,1)S(1)}, u32[]{:S(2)}, u32[]{:S(2)}) async-start(bf16[16,8,1024]{2,1,0:T(8,128)(2,1)} %broadcast_in_dim.48), calls=%async_computation.2 | async-start | bytes 524288 | tf_op jit(solution)/shard_map/all_to_all | solution.py:32
Sparse Core Ops, SparseCore 0:
  16.3 66.8 reduce-scatter.1

commit v2 on v1

v2 whole, which is shorter than its diff:
```python
import jax
import jax.numpy as jnp
from jax import lax
from jax.sharding import PartitionSpec as P

BF16 = jnp.bfloat16
F32 = jnp.float32


def weigh_points(right_basis, point_weight, shell_index, green_table):
    shells_count = green_table.shape[0]
    matches = shell_index[:, None] == jnp.arange(shells_count, dtype=jnp.int32)[None, :]
    green_real = jnp.sum(jnp.where(matches, green_table[None, :, 0], 0.0), axis=1)
    green_imag = jnp.sum(jnp.where(matches, green_table[None, :, 1], 0.0), axis=1)
    weight_real = point_weight * green_real
    weight_imag = point_weight * green_imag
    basis_real = right_basis[0].astype(F32)
    basis_imag = right_basis[1].astype(F32)
    weighted_real = (weight_real[:, None] * basis_real - weight_imag[:, None] * basis_imag).astype(BF16)
    weighted_imag = (weight_real[:, None] * basis_imag + weight_imag[:, None] * basis_real).astype(BF16)
    return (weighted_real, weighted_imag)


def exchange(blocks, axes):
    return lax.all_to_all(blocks, axes, 0, 0, tiled=False)


def dot(a, b):
    return jnp.dot(a, b, preferred_element_type=F32)


def swap(block, bit):
    count = lax.axis_size("row")
    return lax.ppermute(block, "row", [(i, i ^ bit) for i in range(count)])


def pick(blocks, index, axis):
    return lax.dynamic_index_in_dim(blocks, index, axis, keepdims=False)


def ordered(mine, theirs, side):
    return jnp.where(side == 0, jnp.stack([mine, theirs]), jnp.stack([theirs, mine]))


def complex_block(real_part, imag_part):
    upper_half = jnp.concatenate([real_part, imag_part], axis=1)
    lower_half = jnp.concatenate([-imag_part, real_part], axis=1)
    return jnp.concatenate([upper_half, lower_half], axis=0)


def forward(value, sends):
    arrived = [lax.ppermute(value, "col", pairs) for pairs in sends]
    return value + arrived[0] + arrived[1] + arrived[2]


FIRST_SENDS = (((0, 8),), ((0, 2),), ((0, 6),))
SECOND_SENDS = (
    ((0, 1), (8, 9), (2, 10), (6, 14)),
    ((0, 7), (8, 15), (2, 3), (6, 5)),
    ((0, 4), (8, 12), (2, 11), (6, 13)),
)


def body(left_basis, right_basis, point_weight, shell_index, green_table, pivot_rows, diag_inverse):
    shells = lax.axis_size("shell")
    tile_rows = left_basis.shape[1]
    owned_rows = tile_rows // shells
    width = right_basis.shape[2]
    pivots_count = pivot_rows.shape[0]
    grid_row = lax.axis_index("row")
    core, chip = grid_row % 2, grid_row // 2
    weighted_real, weighted_imag = weigh_points(right_basis, point_weight, shell_index, green_table)
    left_stack = jnp.concatenate([left_basis[0], left_basis[1]], axis=1)
    terms = dot(left_stack, complex_block(weighted_real, weighted_imag)).astype(BF16)
    tile_sums = lax.psum_scatter(terms, "shell", scatter_dimension=0, tiled=True)

    tile_index = lax.broadcasted_iota(jnp.int32, (pivots_count, tile_rows), 1) + grid_row * tile_rows
    chosen = (pivot_rows[:, None] == tile_index).astype(BF16)
    picked = dot(chosen, terms).astype(BF16)
    picked = picked.reshape(2, pivots_count // 2, 2 * width)
    picked = pick(picked, core, 0) + swap(pick(picked, 1 - core, 0), 1)
    share_rows = pivots_count // (4 * shells)
    picked = picked.reshape(shells, 2, share_rows, 2 * width)
    picked = pick(picked, chip, 1) + swap(pick(picked, 1 - chip, 1), 2)
    shares = exchange(picked, "shell")
    share = jnp.sum(shares.astype(F32), axis=0).astype(BF16)
    pair = ordered(share, swap(share, 2), chip)
    half = exchange(jnp.broadcast_to(pair[None], (shells,) + pair.shape), "shell").reshape(pivots_count // 2, 2 * width)
    panel = jnp.where(lax.axis_index("col") == 0, tile_sums, jnp.zeros_like(tile_sums))
    panel = forward(panel, FIRST_SENDS)
    half, panel = lax.optimization_barrier((half, panel))
    panel = forward(panel, SECOND_SENDS)
    pivots = jnp.concatenate([half, swap(half, 1)], axis=0)

    side = pivots_count // 2
    turned = jnp.concatenate([diag_inverse[:, :, side:], diag_inverse[:, :, :side]], axis=2)
    inverse = jnp.where(core == 0, diag_inverse, turned)
    inverse_block = jnp.concatenate([inverse[0], inverse[1]], axis=1)
    solved = dot(
        inverse_block,
        jnp.concatenate(
            [pivots, jnp.concatenate([-pivots[:, width:], pivots[:, :width]], axis=1)],
            axis=0,
        ),
    )
    coarse = lax.reduce_precision(solved, 8, 7)
    fine = (solved - coarse).astype(BF16)
    coarse = coarse.astype(BF16)
    turn = lambda block: jnp.concatenate([-block[:, width:], block[:, :width]], axis=1)
    updated = tile_sums.astype(F32) - dot(
        jnp.concatenate([panel, panel], axis=1),
        jnp.concatenate([coarse, turn(coarse), fine, turn(fine)], axis=0),
    )
    return jnp.stack([updated[:, :width], updated[:, width:]]).reshape(2, 1, 1, owned_rows, width)


def solution(mesh):
    return jax.shard_map(
        body,
        mesh=mesh,
        in_specs=(
            P(None, "row", "shell"),
            P(None, "shell", "col"),
            P("shell"),
            P("shell"),
            P(),
            P(),
            P(),
        ),
        out_specs=P(None, "row", "shell", None, "col"),
        check_vma=False,
    )
```

time: 168 us -> 116 us (0.69)
  the two profiles are of different devices: /device:TPU:14 before, /device:TPU:26 now
where the time goes in v2:
time: 116 us
  waiting for transfers between devices  37.2 us (32%)
  blocking collectives  25.2 us (22%)
  starting transfers between devices  20.3 us (18%)
  between operations  13.8 us (12%)
  matrix products  9.68 us (8%)
  other arithmetic  6.7 us (6%)
  local copies, waits for them, and re-layouts  3.04 us (3%)
    all_to_all x1, blocking collectives, exchange(): return lax.all_to_all(blocks, axes, 0, 0, tiled=False)  25.2 us
    ppermute x6, waiting for transfers between devices, forward(): arrived = [lax.ppermute(value, 'col', pairs) for pairs in sends]  13.9 us
    ppermute x4, waiting for transfers between devices, swap(): return lax.ppermute(block, 'row', [(i, i ^ bit) for i in range(count)])  12.8 us
    ppermute x4, starting transfers between devices, swap(): return lax.ppermute(block, 'row', [(i, i ^ bit) for i in range(count)])  12 us
    all_to_all x1, waiting for transfers between devices, exchange(): return lax.all_to_all(blocks, axes, 0, 0, tiled=False)  10.4 us
    dot_general x4, matrix products, dot(): return jnp.dot(a, b, preferred_element_type=F32)  9.68 us
    ppermute x6, starting transfers between devices, forward(): arrived = [lax.ppermute(value, 'col', pairs) for pairs in sends]  4.8 us
    all_to_all x1, starting transfers between devices, exchange(): return lax.all_to_all(blocks, axes, 0, 0, tiled=False)  3.49 us
  transfers between devices with their start and end apart: 12, of which 5 were waited for; matrix products, arithmetic and copies ran while one was open for 5% of the time, Pallas kernels for 0%

profile of v2, /device:TPU:26, one launch (start us, length us, event | category | flops | bytes accessed | tf_op | source)
XLA Modules:
  0.0 115.9 jit_solution(876430515374612148)
XLA Ops:
  6.5 0.8 slice_bitcast_fusion.6
  7.4 1.2 %select_reduce_fusion.1 = (f32[768]{0:T(1024)S(1)}, f32[768]{0:T(1024)S(1)}) fusion(f32[12]{0:T(128)S(1)} %get-tuple-element.32, s32[768]{0:T(1024)} %param.10, f32[12]{0:T(128)S(1)} %get-tuple-element.31), kind=kLoop, calls=%fused_computation.75 | loop fusion | flops 44544 | bytes 9312 | tf_op jit(solution)/shard_map/reduce_sum | solution.py:13
  8.6 0.7 fusion.63
  9.3 1.8 %fusion.60 = (bf16[768,512]{1,0:T(8,128)(2,1)S(1)}, bf16[768,512]{1,0:T(8,128)(2,1)S(1)}) fusion(bf16[2,768,512]{2,1,0:T(8,128)(2,1)} %param.8, f32[768]{0:T(1024)S(1)} %get-tuple-element.30, f32[768]{0:T(1024)S(1)} %get-tuple-element.29), kind=kLoop, calls=%fused_computation.85 | loop fusion | flops 2752512 | bytes 3151872 | tf_op jit(solution)/shard_map/neg | solution.py:47
  11.1 0.4 fusion.40
  11.5 0.2 slice_bitcast_fusion.1
  11.7 4.7 %fusion.34 = bf16[1024,1024]{1,0:T(8,128)(2,1)} fusion(bf16[768,512]{1,0:T(8,128)(2,1)S(1)} %fusion.40, bf16[768,512]{1,0:T(8,128)(2,1)S(1)} %get-tuple-element.11, bf16[768,512]{1,0:T(8,128)(2,1)S(1)} %get-tuple-element.12, bf16[1024,768]{1,0:T(8,128)(2,1)S(1)} %get-tuple-element.14, bf16[1024,768]{1,0:T(8,128)(2,1)S(1)} %get-tuple-element.13), kind=kOutput, calls=%fused_computation.40 | convolution fusion | flops 3241148416 | bytes 7602176 | tf_op jit(solution)/shard_map/dot_general | solution.py:29
  16.6 2.9 %fusion.43 = bf16[512,1024]{1,0:T(8,128)(2,1)S(1)} fusion(bf16[1024,1024]{1,0:T(8,128)(2,1)} %fusion.34, s32[1024]{0:T(1024)S(1)} %iota_add_fusion, s32[512]{0:T(512)S(1)} %copy-done.4), kind=kOutput, calls=%fused_computation.47 | convolution fusion | flops 1074790400 | bytes 3151872 | tf_op jit(solution)/shard_map/dot_general | solution.py:29
  19.5 2.1 %collective-permute-start = (bf16[256,1024]{1,0:T(8,128)(2,1)S(1)}, bf16[256,1024]{1,0:T(8,128)(2,1)S(1)}, u32[]{:S(2)}, u32[]{:S(2)}) collective-permute-start(bf16[256,1024]{1,0:T(8,128)(2,1)S(1)} %dynamic-slice_bitcast_fusion), channel_id=1, source_target_pairs={{0,16},{16,0},{32,48},{48,32},{1,17},{17,1},{33,49},{49,33},{2,18}... | collective-permute-start | bytes 1572872 | tf_op jit(solution)/shard_map/ppermute | solution.py:34
  21.6 1.8 %collective-permute-done = bf16[256,1024]{1,0:T(8,128)(2,1)S(1)} collective-permute-done((bf16[256,1024]{1,0:T(8,128)(2,1)S(1)}, bf16[256,1024]{1,0:T(8,128)(2,1)S(1)}, u32[]{:S(2)}, u32[]{:S(2)}) %collective-permute-start) | collective-permute-done | bytes 524320 | tf_op jit(solution)/shard_map/ppermute | solution.py:34
  23.5 4.0 %collective-permute-start.1 = (bf16[8,16,1024]{2,1,0:T(8,128)(2,1)S(1)}, bf16[8,16,1024]{2,1,0:T(8,128)(2,1)S(1)}, u32[]{:S(2)}, u32[]{:S(2)}) collective-permute-start(bf16[8,16,1024]{2,1,0:T(8,128)(2,1)S(1)} %dynamic-slice_bitcast_fusion.1), channel_id=1, source_target_pairs={{0,32},{16,48},{32,0},{48,16},{1,33},{17,49},{33,1},{49,17},{2,34}... | collective-permute-start | bytes 786440 | tf_op jit(solution)/shard_map/ppermute | solution.py:34
  27.6 7.7 %collective-permute-done.1 = bf16[8,16,1024]{2,1,0:T(8,128)(2,1)S(1)} collective-permute-done((bf16[8,16,1024]{2,1,0:T(8,128)(2,1)S(1)}, bf16[8,16,1024]{2,1,0:T(8,128)(2,1)S(1)}, u32[]{:S(2)}, u32[]{:S(2)}) %collective-permute-start.1) | collective-permute-done | bytes 262176 | tf_op jit(solution)/shard_map/ppermute | solution.py:34
  35.3 25.2 %all_to_all.10 = bf16[8,16,1024]{2,1,0:T(8,128)(2,1)S(1)} all-to-all(bf16[8,16,1024]{2,1,0:T(8,128)(2,1)S(1)} %bitcast_add_fusion.1), channel_id=1, replica_groups=mesh['shell'=8,'row'=4,'col'=16] {'shell'}, dimensions={0} | all-to-all | bytes 524288 | tf_op jit(solution)/shard_map/all_to_all | solution.py:25
  60.5 4.0 %collective-permute-start.2 = (bf16[16,1024]{1,0:T(8,128)(2,1)S(1)}, bf16[16,1024]{1,0:T(8,128)(2,1)S(1)}, u32[]{:S(2)}, u32[]{:S(2)}) collective-permute-start(bf16[16,1024]{1,0:T(8,128)(2,1)S(1)} %reduce_sum.32), channel_id=1, source_target_pairs={{0,32},{16,48},{32,0},{48,16},{1,33},{17,49},{33,1},{49,17},{2,34}... | collective-permute-start | bytes 98312 | tf_op jit(solution)/shard_map/ppermute | solution.py:34
  64.6 3.3 %collective-permute-done.2 = bf16[16,1024]{1,0:T(8,128)(2,1)S(1)} collective-permute-done((bf16[16,1024]{1,0:T(8,128)(2,1)S(1)}, bf16[16,1024]{1,0:T(8,128)(2,1)S(1)}, u32[]{:S(2)}, u32[]{:S(2)}) %collective-permute-start.2) | collective-permute-done | bytes 32800 | tf_op jit(solution)/shard_map/ppermute | solution.py:34
  67.9 0.9 broadcast_in_dim.43
  68.7 3.5 %all-to-all-start.1 = ((bf16[8,2,16,1024]{3,2,1,0:T(8,128)(2,1)}), bf16[8,2,16,1024]{3,2,1,0:T(8,128)(2,1)S(1)}, u32[]{:S(2)}, u32[]{:S(2)}) async-start(bf16[8,2,16,1024]{3,2,1,0:T(8,128)(2,1)} %broadcast_in_dim.43), calls=%async_computation.2 | async-start | bytes 1048576 | tf_op jit(solution)/shard_map/all_to_all | solution.py:25
  72.2 0.9 fusion.62
  73.1 0.8 collective-permute-start.3
  73.9 0.7 collective-permute-start.4
  74.6 0.7 collective-permute-start.5
  75.3 1.3 %maximum_select_fusion = bf16[2,512,512]{2,1,0:T(8,128)(2,1)S(1)} fusion(bf16[2,512,512]{2,1,0:T(8,128)(2,1)S(1)} %copy-done.1, bf16[2,512,256]{2,1,0:T(8,128)(2,1)} %get-tuple-element.24, bf16[2,512,256]{2,1,0:T(8,128)(2,1)S(1)} %get-tuple-element.23, pred[]{:T(512)S(6)} %eq.39), kind=kLoop, calls=%fused_computation.49 | loop fusion | flops 2621440 | bytes 3145729 | tf_op jit(solution)/shard_map/jit(_where)/select_n | solution.py:97
  76.7 10.4 %all-to-all-done.1 = bf16[8,2,16,1024]{3,2,1,0:T(8,128)(2,1)S(1)} async-done(((bf16[8,2,16,1024]{3,2,1,0:T(8,128)(2,1)}), bf16[8,2,16,1024]{3,2,1,0:T(8,128)(2,1)S(1)}, u32[]{:S(2)}, u32[]{:S(2)}) %all-to-all-start.1) | async-done | bytes 524320 | tf_op jit(solution)/shard_map/all_to_all | solution.py:25
  87.1 0.7 collective-permute-start.6
  87.8 0.7 collective-permute-start.7
  88.5 1.3 %collective-permute-start.8 = (bf16[128,1024]{1,0:T(8,128)(2,1)S(1)}, bf16[128,1024]{1,0:T(8,128)(2,1)S(1)}, u32[]{:S(2)}, u32[]{:S(2)}) collective-permute-start(bf16[128,1024]{1,0:T(8,128)(2,1)S(1)} %add_add_fusion.1), channel_id=1, source_target_pairs={{0,4},{8,12},{2,11},{6,13},{16,20},{24,28},{18,27},{22,29},{32,36}... | collective-permute-start | bytes 786440 | tf_op jit(solution)/shard_map/ppermute | solution.py:52
  89.8 1.9 %collective-permute-start.9 = (bf16[256,1024]{1,0:T(8,128)(2,1)S(1)}, bf16[256,1024]{1,0:T(8,128)(2,1)S(1)}, u32[]{:S(2)}, u32[]{:S(2)}) collective-permute-start(bf16[256,1024]{1,0:T(8,128)(2,1)S(1)} %bitcast.44), channel_id=1, source_target_pairs={{0,16},{16,0},{32,48},{48,32},{1,17},{17,1},{33,49},{49,33},{2,18}... | collective-permute-start | bytes 1572872 | tf_op jit(solution)/shard_map/ppermute | solution.py:34
  91.8 13.9 %collective-permute-done.8 = bf16[128,1024]{1,0:T(8,128)(2,1)S(1)} collective-permute-done((bf16[128,1024]{1,0:T(8,128)(2,1)S(1)}, bf16[128,1024]{1,0:T(8,128)(2,1)S(1)}, u32[]{:S(2)}, u32[]{:S(2)}) %collective-permute-start.8) | collective-permute-done | bytes 262176 | tf_op jit(solution)/shard_map/ppermute | solution.py:52
  106.0 1.3 %reduce-precision_convert_fusion = (bf16[512,1024]{1,0:T(8,128)(2,1)S(1)}, bf16[512,1024]{1,0:T(8,128)(2,1)S(1)}) fusion(bf16[512,512]{1,0:T(8,128)(2,1)S(1)} %get-tuple-element.26, bf16[512,512]{1,0:T(8,128)(2,1)S(1)} %get-tuple-element.25, bf16[256,1024]{1,0:T(8,128)(2,1)S(1)} %collective-permute-done.9, bf16[256,1024]{1,0:T(8,128)(2,1)S(1)} %bitcast.46, ...), kind=kOutput, calls=%fused_computation.24 | convolution fusion | flops 1086324736 | bytes 5242880 | tf_op jit(solution)/shard_map/dot_general | solution.py:29
  107.3 0.1 slice_negate_fusion
  107.4 0.8 fusion.46
  108.2 0.8 maximum_bitcast_fusion
  (34 shorter events, 0.6 us)
Async XLA Ops:
  6.5 4.6 %copy-start = (bf16[2,768,512]{2,1,0:T(8,128)(2,1)S(1)}, bf16[2,768,512]{2,1,0:T(8,128)(2,1)}, u32[]{:S(2)}) copy-start(bf16[2,768,512]{2,1,0:T(8,128)(2,1)} %param.8) | copy-start | bytes 4718596
  6.5 66.6 %reduce-scatter.2.cloned.1.call-start = ((), (), s32[]{:S(2)}) async-start(), calls=%async_computation.3 | async-start | bytes 2359296 | tf_op jit(solution)/shard_map/reduce_scatter | solution.py:75
  6.5 5.0 %copy-start.2 = (bf16[2,1024,768]{2,1,0:T(8,128)(2,1)S(1)}, bf16[2,1024,768]{2,1,0:T(8,128)(2,1)}, u32[]{:S(2)}) copy-start(bf16[2,1024,768]{2,1,0:T(8,128)(2,1)} %param.7) | copy-start | bytes 9437188
  11.7 4.8 %copy-start.4 = (s32[512]{0:T(512)S(1)}, s32[512]{0:T(512)}, u32[]{:S(2)}) copy-start(s32[512]{0:T(512)} %param.12) | copy-start | bytes 6148
  19.4 52.8 %copy-start.1 = (bf16[2,512,512]{2,1,0:T(8,128)(2,1)S(1)}, bf16[2,512,512]{2,1,0:T(8,128)(2,1)}, u32[]{:S(2)}) copy-start(bf16[2,512,512]{2,1,0:T(8,128)(2,1)} %param.13) | copy-start | bytes 3145732
  19.5 3.9 %collective-permute-start = (bf16[256,1024]{1,0:T(8,128)(2,1)S(1)}, bf16[256,1024]{1,0:T(8,128)(2,1)S(1)}, u32[]{:S(2)}, u32[]{:S(2)}) collective-permute-start(bf16[256,1024]{1,0:T(8,128)(2,1)S(1)} %dynamic-slice_bitcast_fusion), channel_id=1, source_target_pairs={{0,16},{16,0},{32,48},{48,32},{1,17},{17,1},{33,49},{49,33},{2,18}... | collective-permute-start | bytes 1572872 | tf_op jit(solution)/shard_map/ppermute | solution.py:34
  23.5 11.7 %collective-permute-start.1 = (bf16[8,16,1024]{2,1,0:T(8,128)(2,1)S(1)}, bf16[8,16,1024]{2,1,0:T(8,128)(2,1)S(1)}, u32[]{:S(2)}, u32[]{:S(2)}) collective-permute-start(bf16[8,16,1024]{2,1,0:T(8,128)(2,1)S(1)} %dynamic-slice_bitcast_fusion.1), channel_id=1, source_target_pairs={{0,32},{16,48},{32,0},{48,16},{1,33},{17,49},{33,1},{49,17},{2,34}... | collective-permute-start | bytes 786440 | tf_op jit(solution)/shard_map/ppermute | solution.py:34
  60.5 7.3 %collective-permute-start.2 = (bf16[16,1024]{1,0:T(8,128)(2,1)S(1)}, bf16[16,1024]{1,0:T(8,128)(2,1)S(1)}, u32[]{:S(2)}, u32[]{:S(2)}) collective-permute-start(bf16[16,1024]{1,0:T(8,128)(2,1)S(1)} %reduce_sum.32), channel_id=1, source_target_pairs={{0,32},{16,48},{32,0},{48,16},{1,33},{17,49},{33,1},{49,17},{2,34}... | collective-permute-start | bytes 98312 | tf_op jit(solution)/shard_map/ppermute | solution.py:34
  68.7 18.4 %all-to-all-start.1 = ((bf16[8,2,16,1024]{3,2,1,0:T(8,128)(2,1)}), bf16[8,2,16,1024]{3,2,1,0:T(8,128)(2,1)S(1)}, u32[]{:S(2)}, u32[]{:S(2)}) async-start(bf16[8,2,16,1024]{3,2,1,0:T(8,128)(2,1)} %broadcast_in_dim.43), calls=%async_computation.2 | async-start | bytes 1048576 | tf_op jit(solution)/shard_map/all_to_all | solution.py:25
  73.1 3.6 %copy-start.3 = (bf16[128,1024]{1,0:T(8,128)(2,1)S(1)}, bf16[128,1024]{1,0:T(8,128)(2,1)}, u32[]{:S(2)}) copy-start(bf16[128,1024]{1,0:T(8,128)(2,1)} %reduce-scatter.2.cloned.1.call-done) | copy-start | bytes 786436
  73.1 3.5 %collective-permute-start.3 = (bf16[128,1024]{1,0:T(8,128)(2,1)S(1)}, bf16[128,1024]{1,0:T(8,128)(2,1)S(1)}, u32[]{:S(2)}, u32[]{:S(2)}) collective-permute-start(bf16[128,1024]{1,0:T(8,128)(2,1)S(1)} %broadcast_select_fusion), channel_id=1, source_target_pairs={{0,8},{16,24},{32,40},{48,56},{64,72},{80,88},{96,104},{112,120},{... | collective-permute-start | bytes 786440 | tf_op jit(solution)/shard_map/ppermute | solution.py:52
  73.9 2.7 %collective-permute-start.4 = (bf16[128,1024]{1,0:T(8,128)(2,1)S(1)}, bf16[128,1024]{1,0:T(8,128)(2,1)S(1)}, u32[]{:S(2)}, u32[]{:S(2)}) collective-permute-start(bf16[128,1024]{1,0:T(8,128)(2,1)S(1)} %broadcast_select_fusion), channel_id=1, source_target_pairs={{0,2},{16,18},{32,34},{48,50},{64,66},{80,82},{96,98},{112,114},{1... | collective-permute-start | bytes 786440 | tf_op jit(solution)/shard_map/ppermute | solution.py:52
  74.6 2.0 %collective-permute-start.5 = (bf16[128,1024]{1,0:T(8,128)(2,1)S(1)}, bf16[128,1024]{1,0:T(8,128)(2,1)S(1)}, u32[]{:S(2)}, u32[]{:S(2)}) collective-permute-start(bf16[128,1024]{1,0:T(8,128)(2,1)S(1)} %broadcast_select_fusion), channel_id=1, source_target_pairs={{0,6},{16,22},{32,38},{48,54},{64,70},{80,86},{96,102},{112,118},{... | collective-permute-start | bytes 786440 | tf_op jit(solution)/shard_map/ppermute | solution.py:52
  87.1 4.7 %collective-permute-start.6 = (bf16[128,1024]{1,0:T(8,128)(2,1)S(1)}, bf16[128,1024]{1,0:T(8,128)(2,1)S(1)}, u32[]{:S(2)}, u32[]{:S(2)}) collective-permute-start(bf16[128,1024]{1,0:T(8,128)(2,1)S(1)} %add_add_fusion.1), channel_id=1, source_target_pairs={{0,1},{8,9},{2,10},{6,14},{16,17},{24,25},{18,26},{22,30},{32,33},... | collective-permute-start | bytes 786440 | tf_op jit(solution)/shard_map/ppermute | solution.py:52
  87.8 4.0 %collective-permute-start.7 = (bf16[128,1024]{1,0:T(8,128)(2,1)S(1)}, bf16[128,1024]{1,0:T(8,128)(2,1)S(1)}, u32[]{:S(2)}, u32[]{:S(2)}) collective-permute-start(bf16[128,1024]{1,0:T(8,128)(2,1)S(1)} %add_add_fusion.1), channel_id=1, source_target_pairs={{0,7},{8,15},{2,3},{6,5},{16,23},{24,31},{18,19},{22,21},{32,39},{... | collective-permute-start | bytes 786440 | tf_op jit(solution)/shard_map/ppermute | solution.py:52
  88.5 17.3 %collective-permute-start.8 = (bf16[128,1024]{1,0:T(8,128)(2,1)S(1)}, bf16[128,1024]{1,0:T(8,128)(2,1)S(1)}, u32[]{:S(2)}, u32[]{:S(2)}) collective-permute-start(bf16[128,1024]{1,0:T(8,128)(2,1)S(1)} %add_add_fusion.1), channel_id=1, source_target_pairs={{0,4},{8,12},{2,11},{6,13},{16,20},{24,28},{18,27},{22,29},{32,36}... | collective-permute-start | bytes 786440 | tf_op jit(solution)/shard_map/ppermute | solution.py:52
  89.8 16.1 %collective-permute-start.9 = (bf16[256,1024]{1,0:T(8,128)(2,1)S(1)}, bf16[256,1024]{1,0:T(8,128)(2,1)S(1)}, u32[]{:S(2)}, u32[]{:S(2)}) collective-permute-start(bf16[256,1024]{1,0:T(8,128)(2,1)S(1)} %bitcast.44), channel_id=1, source_target_pairs={{0,16},{16,0},{32,48},{48,32},{1,17},{17,1},{33,49},{49,33},{2,18}... | collective-permute-start | bytes 1572872 | tf_op jit(solution)/shard_map/ppermute | solution.py:34
Sparse Core Ops, SparseCore 0:
  16.6 53.7 reduce-scatter.1

commit v3 on v2

--- a/solution.py
+++ b/solution.py
@@ -1,24 +1,107 @@
 import jax
 import jax.numpy as jnp
 from jax import lax
+from jax.experimental import pallas as pl
+from jax.experimental.pallas import tpu as pltpu
 from jax.sharding import PartitionSpec as P
 
 BF16 = jnp.bfloat16
 F32 = jnp.float32
 
 
-def weigh_points(right_basis, point_weight, shell_index, green_table):
-    shells_count = green_table.shape[0]
-    matches = shell_index[:, None] == jnp.arange(shells_count, dtype=jnp.int32)[None, :]
-    green_real = jnp.sum(jnp.where(matches, green_table[None, :, 0], 0.0), axis=1)
-    green_imag = jnp.sum(jnp.where(matches, green_table[None, :, 1], 0.0), axis=1)
-    weight_real = point_weight * green_real
-    weight_imag = point_weight * green_imag
-    basis_real = right_basis[0].astype(F32)
-    basis_imag = right_basis[1].astype(F32)
-    weighted_real = (weight_real[:, None] * basis_real - weight_imag[:, None] * basis_imag).astype(BF16)
-    weighted_imag = (weight_real[:, None] * basis_imag + weight_imag[:, None] * basis_real).astype(BF16)
-    return (weighted_real, weighted_imag)
+LANES = 128
+SUBLANES = 8
+ROW_STEPS = 4
+
+
+def terms_kernel(
+    green_ref, weight_ref, index_ref, left_hbm, right_hbm, terms_hbm,
+    left_ref, right_ref, stack_ref, terms_ref, in_sems, out_sems,
+):
+    points, width = right_ref.shape[1], right_ref.shape[2]
+    right_copy = pltpu.make_async_copy(right_hbm, right_ref, in_sems.at[0])
+    left_copy = pltpu.make_async_copy(left_hbm, left_ref, in_sems.at[1])
+    right_copy.start()
+    left_copy.start()
+
+    index = index_ref[...]
+    green_real = jnp.zeros(index.shape, F32)
+    green_imag = jnp.zeros(index.shape, F32)
+    for shell in range(green_ref.shape[1]):
+        match = index == shell
+        green_real = jnp.where(match, green_ref[0, shell], green_real)
+        green_imag = jnp.where(match, green_ref[1, shell], green_imag)
+    groups = index.shape[0]
+    fill = jnp.zeros((-groups % SUBLANES, LANES), F32)
+    weight_real = jnp.transpose(jnp.concatenate([weight_ref[...] * green_real, fill], axis=0))
+    weight_imag = jnp.transpose(jnp.concatenate([weight_ref[...] * green_imag, fill], axis=0))
+    right_copy.wait()
+    for group in range(groups):
+        rows = slice(group * LANES, (group + 1) * LANES)
+        below = slice(points + group * LANES, points + (group + 1) * LANES)
+        factor_real = weight_real[:, group : group + 1]
+        factor_imag = weight_imag[:, group : group + 1]
+        basis_real = right_ref[0, rows, :].astype(F32)
+        basis_imag = right_ref[1, rows, :].astype(F32)
+        real = (factor_real * basis_real - factor_imag * basis_imag).astype(BF16)
+        imag = (factor_real * basis_imag + factor_imag * basis_real).astype(BF16)
+        stack_ref[rows, :width] = real
+        stack_ref[rows, width:] = imag
+        stack_ref[below, :width] = -imag
+        stack_ref[below, width:] = real
+
+    left_copy.wait()
+    step_rows = left_ref.shape[1] // ROW_STEPS
+    copies = []
+    for step in range(ROW_STEPS):
+        rows = slice(step * step_rows, (step + 1) * step_rows)
+        total = jnp.dot(left_ref[0, rows, :], stack_ref[:points, :], preferred_element_type=F32)
+        total = total + jnp.dot(left_ref[1, rows, :], stack_ref[points:, :], preferred_element_type=F32)
+        terms_ref[rows, :] = total.astype(BF16)
+        copy = pltpu.make_async_copy(
+            terms_ref.at[pl.ds(step * step_rows, step_rows), :],
+            terms_hbm.at[pl.ds(step * step_rows, step_rows), :],
+            out_sems.at[step],
+        )
+        copy.start()
+        copies.append(copy)
+    for copy in copies:
+        copy.wait()
+
+
+def partial_terms(left_basis, right_basis, point_weight, shell_index, green_table):
+    _, tile_rows, points = left_basis.shape
+    width = right_basis.shape[2]
+    groups = points // LANES
+    in_vmem = pl.BlockSpec(memory_space=pltpu.VMEM)
+    in_hbm = pl.BlockSpec(memory_space=pltpu.HBM)
+    return pl.pallas_call(
+        terms_kernel,
+        in_specs=[pl.BlockSpec(memory_space=pltpu.SMEM), in_vmem, in_vmem, in_hbm, in_hbm],
+        out_specs=in_hbm,
+        out_shape=jax.ShapeDtypeStruct((tile_rows, 2 * width), BF16),
+        scratch_shapes=[
+            pltpu.VMEM(left_basis.shape, BF16),
+            pltpu.VMEM(right_basis.shape, BF16),
+            pltpu.VMEM((2 * points, 2 * width), BF16),
+            pltpu.VMEM((tile_rows, 2 * width), BF16),
+            pltpu.SemaphoreType.DMA((2,)),
+            pltpu.SemaphoreType.DMA((ROW_STEPS,)),
+        ],
+        compiler_params=pltpu.CompilerParams(vmem_limit_bytes=62 * 1024 * 1024),
+        cost_estimate=pl.CostEstimate(
+            flops=8 * tile_rows * points * width,
+            transcendentals=0,
+            bytes_accessed=2 * (left_basis.size + right_basis.size + 2 * tile_rows * width),
+        ),
+        name="terms",
+    )(
+        green_table.T,
+        point_weight.reshape(groups, LANES),
+        shell_index.reshape(groups, LANES),
+        left_basis,
+        right_basis,
+    )
 
 
 def exchange(blocks, axes):
@@ -42,12 +125,6 @@
     return jnp.where(side == 0, jnp.stack([mine, theirs]), jnp.stack([theirs, mine]))
 
 
-def complex_block(real_part, imag_part):
-    upper_half = jnp.concatenate([real_part, imag_part], axis=1)
-    lower_half = jnp.concatenate([-imag_part, real_part], axis=1)
-    return jnp.concatenate([upper_half, lower_half], axis=0)
-
-
 def forward(value, sends):
     arrived = [lax.ppermute(value, "col", pairs) for pairs in sends]
     return value + arrived[0] + arrived[1] + arrived[2]
@@ -55,9 +132,9 @@
 
 FIRST_SENDS = (((0, 8),), ((0, 2),), ((0, 6),))
 SECOND_SENDS = (
-    ((0, 1), (8, 9), (2, 10), (6, 14)),
-    ((0, 7), (8, 15), (2, 3), (6, 5)),
-    ((0, 4), (8, 12), (2, 11), (6, 13)),
+    ((0, 9), (8, 11), (2, 4), (6, 12)),
+    ((0, 7), (8, 13), (2, 10), (6, 14)),
+    ((0, 1), (8, 15), (2, 3), (6, 5)),
 )
 
 
@@ -69,9 +146,7 @@
     pivots_count = pivot_rows.shape[0]
     grid_row = lax.axis_index("row")
     core, chip = grid_row % 2, grid_row // 2
-    weighted_real, weighted_imag = weigh_points(right_basis, point_weight, shell_index, green_table)
-    left_stack = jnp.concatenate([left_basis[0], left_basis[1]], axis=1)
-    terms = dot(left_stack, complex_block(weighted_real, weighted_imag)).astype(BF16)
+    terms = partial_terms(left_basis, right_basis, point_weight, shell_index, green_table)
     tile_sums = lax.psum_scatter(terms, "shell", scatter_dimension=0, tiled=True)
 
     tile_index = lax.broadcasted_iota(jnp.int32, (pivots_count, tile_rows), 1) + grid_row * tile_rows
@@ -88,7 +163,7 @@
     half = exchange(jnp.broadcast_to(pair[None], (shells,) + pair.shape), "shell").reshape(pivots_count // 2, 2 * width)
     panel = jnp.where(lax.axis_index("col") == 0, tile_sums, jnp.zeros_like(tile_sums))
     panel = forward(panel, FIRST_SENDS)
-    half, panel = lax.optimization_barrier((half, panel))
+    half, _ = lax.optimization_barrier((half, panel))
     panel = forward(panel, SECOND_SENDS)
     pivots = jnp.concatenate([half, swap(half, 1)], axis=0)
 

time: 116 us -> 105 us (0.905)
  the two profiles are of different devices: /device:TPU:26 before, /device:TPU:14 now
where the time goes in v3:
time: 105 us
  waiting for transfers between devices  28 us (27%)
  blocking collectives  25.1 us (24%)
  starting transfers between devices  19.6 us (19%)
  between operations  13.8 us (13%)
  Pallas kernels  7.5 us (7%)
  matrix products  4.91 us (5%)
  other arithmetic  3.65 us (3%)
  local copies, waits for them, and re-layouts  1.99 us (2%)
    all_to_all x1, blocking collectives, exchange(): return lax.all_to_all(blocks, axes, 0, 0, tiled=False)  25.1 us
    ppermute x4, waiting for transfers between devices, swap(): return lax.ppermute(block, 'row', [(i, i ^ bit) for i in range(count)])  14.2 us
    ppermute x4, starting transfers between devices, swap(): return lax.ppermute(block, 'row', [(i, i ^ bit) for i in range(count)])  10.7 us
    pallas_call x1, Pallas kernels, partial_terms(): pl.pallas_call(terms_kernel, in_specs=[pl.BlockSpec(memory_space=pltpu.SM...  7.5 us
    ppermute x6, waiting for transfers between devices, forward(): arrived = [lax.ppermute(value, 'col', pairs) for pairs in sends]  6.93 us
    all_to_all x1, waiting for transfers between devices, exchange(): return lax.all_to_all(blocks, axes, 0, 0, tiled=False)  6.91 us
    ppermute x6, starting transfers between devices, forward(): arrived = [lax.ppermute(value, 'col', pairs) for pairs in sends]  5.5 us
    dot_general x3, matrix products, dot(): return jnp.dot(a, b, preferred_element_type=F32)  4.91 us
  transfers between devices with their start and end apart: 12, of which 5 were waited for; matrix products, arithmetic and copies ran while one was open for 7% of the time, Pallas kernels for 0%

profile of v3, /device:TPU:14, one launch (start us, length us, event | category | flops | bytes accessed | tf_op | source)
XLA Modules:
  0.0 104.6 jit_solution(11977526365527782102)
XLA Ops:
  6.5 7.5 %terms.1 = bf16[1024,1024]{1,0:T(8,128)(2,1)} custom-call(f32[2,12]{1,0:T(2,128)} %bitcast.40, f32[6,128]{1,0:T(8,128)} %bitcast.38, s32[6,128]{1,0:T(8,128)} %bitcast.39, bf16[2,1024,768]{2,1,0:T(8,128)(2,1)} %left_hbm.1, bf16[2,768,512]{2,1,0:T(8,128)(2,1)} %right_hbm.1), custom_call_target="tpu_custom_call" | custom-call | flops 3221225472 | bytes 6815744 | tf_op jit(solution)/shard_map/terms/pallas_call | solution.py:78
  14.1 0.0 reduce-scatter.2.cloned.1.call-update
  14.1 2.9 %fusion.23 = bf16[512,1024]{1,0:T(8,128)(2,1)S(1)} fusion(bf16[1024,1024]{1,0:T(8,128)(2,1)} %terms.1, s32[1024]{0:T(1024)S(1)} %iota_add_fusion, s32[512]{0:T(512)S(1)} %copy-done.2), kind=kOutput, calls=%fused_computation.25 | convolution fusion | flops 1074790400 | bytes 3151872 | tf_op jit(solution)/shard_map/dot_general | solution.py:112
  17.1 2.1 %collective-permute-start.6 = (bf16[256,1024]{1,0:T(8,128)(2,1)S(1)}, bf16[256,1024]{1,0:T(8,128)(2,1)S(1)}, u32[]{:S(2)}, u32[]{:S(2)}) collective-permute-start(bf16[256,1024]{1,0:T(8,128)(2,1)S(1)} %dynamic-slice_bitcast_fusion), channel_id=1, source_target_pairs={{0,16},{16,0},{32,48},{48,32},{1,17},{17,1},{33,49},{49,33},{2,18}... | collective-permute-start | bytes 1572872 | tf_op jit(solution)/shard_map/ppermute | solution.py:117
  19.2 1.8 %collective-permute-done.6 = bf16[256,1024]{1,0:T(8,128)(2,1)S(1)} collective-permute-done((bf16[256,1024]{1,0:T(8,128)(2,1)S(1)}, bf16[256,1024]{1,0:T(8,128)(2,1)S(1)}, u32[]{:S(2)}, u32[]{:S(2)}) %collective-permute-start.6) | collective-permute-done | bytes 524320 | tf_op jit(solution)/shard_map/ppermute | solution.py:117
  21.0 0.1 bitcast_add_fusion
  21.1 3.3 %collective-permute-start.7 = (bf16[8,16,1024]{2,1,0:T(8,128)(2,1)S(1)}, bf16[8,16,1024]{2,1,0:T(8,128)(2,1)S(1)}, u32[]{:S(2)}, u32[]{:S(2)}) collective-permute-start(bf16[8,16,1024]{2,1,0:T(8,128)(2,1)S(1)} %dynamic-slice_bitcast_fusion.1), channel_id=1, source_target_pairs={{0,32},{16,48},{32,0},{48,16},{1,33},{17,49},{33,1},{49,17},{2,34}... | collective-permute-start | bytes 786440 | tf_op jit(solution)/shard_map/ppermute | solution.py:117
  24.4 8.4 %collective-permute-done.7 = bf16[8,16,1024]{2,1,0:T(8,128)(2,1)S(1)} collective-permute-done((bf16[8,16,1024]{2,1,0:T(8,128)(2,1)S(1)}, bf16[8,16,1024]{2,1,0:T(8,128)(2,1)S(1)}, u32[]{:S(2)}, u32[]{:S(2)}) %collective-permute-start.7) | collective-permute-done | bytes 262176 | tf_op jit(solution)/shard_map/ppermute | solution.py:117
  32.9 25.1 %all_to_all.10 = bf16[8,16,1024]{2,1,0:T(8,128)(2,1)S(1)} all-to-all(bf16[8,16,1024]{2,1,0:T(8,128)(2,1)S(1)} %bitcast_add_fusion.1), channel_id=1, replica_groups=mesh['shell'=8,'row'=4,'col'=16] {'shell'}, dimensions={0} | all-to-all | bytes 524288 | tf_op jit(solution)/shard_map/all_to_all | solution.py:108
  58.1 3.4 %collective-permute-start.8 = (bf16[16,1024]{1,0:T(8,128)(2,1)S(1)}, bf16[16,1024]{1,0:T(8,128)(2,1)S(1)}, u32[]{:S(2)}, u32[]{:S(2)}) collective-permute-start(bf16[16,1024]{1,0:T(8,128)(2,1)S(1)} %reduce_sum.12), channel_id=1, source_target_pairs={{0,32},{16,48},{32,0},{48,16},{1,33},{17,49},{33,1},{49,17},{2,34}... | collective-permute-start | bytes 98312 | tf_op jit(solution)/shard_map/ppermute | solution.py:117
  61.5 3.9 %collective-permute-done.8 = bf16[16,1024]{1,0:T(8,128)(2,1)S(1)} collective-permute-done((bf16[16,1024]{1,0:T(8,128)(2,1)S(1)}, bf16[16,1024]{1,0:T(8,128)(2,1)S(1)}, u32[]{:S(2)}, u32[]{:S(2)}) %collective-permute-start.8) | collective-permute-done | bytes 32800 | tf_op jit(solution)/shard_map/ppermute | solution.py:117
  65.4 0.9 broadcast_in_dim.5
  66.2 3.5 %all-to-all-start.1 = ((bf16[8,2,16,1024]{3,2,1,0:T(8,128)(2,1)}), bf16[8,2,16,1024]{3,2,1,0:T(8,128)(2,1)S(1)}, u32[]{:S(2)}, u32[]{:S(2)}) async-start(bf16[8,2,16,1024]{3,2,1,0:T(8,128)(2,1)} %broadcast_in_dim.5), calls=%async_computation.2 | async-start | bytes 1048576 | tf_op jit(solution)/shard_map/all_to_all | solution.py:108
  69.8 0.9 fusion.39
  70.7 0.8 collective-permute-start.1
  71.5 0.7 collective-permute-start.2
  72.2 0.7 collective-permute-start
  72.8 1.3 %maximum_select_fusion = bf16[2,512,512]{2,1,0:T(8,128)(2,1)S(1)} fusion(bf16[2,512,512]{2,1,0:T(8,128)(2,1)S(1)} %copy-done, bf16[2,512,256]{2,1,0:T(8,128)(2,1)} %get-tuple-element.16, bf16[2,512,256]{2,1,0:T(8,128)(2,1)S(1)} %get-tuple-element.15, pred[]{:T(512)S(6)} %eq.20), kind=kLoop, calls=%fused_computation.27 | loop fusion | flops 2621440 | bytes 3145729 | tf_op jit(solution)/shard_map/jit(_where)/select_n | solution.py:172
  74.2 0.1 add_add_fusion.1
  74.3 0.7 collective-permute-start.5
  74.9 1.4 %collective-permute-start.4 = (bf16[128,1024]{1,0:T(8,128)(2,1)S(1)}, bf16[128,1024]{1,0:T(8,128)(2,1)}, u32[]{:S(2)}, u32[]{:S(2)}) collective-permute-start(bf16[128,1024]{1,0:T(8,128)(2,1)S(1)} %add_add_fusion.1), channel_id=1, source_target_pairs={{0,7},{8,13},{2,10},{6,14},{16,23},{24,29},{18,26},{22,30},{32,39}... | collective-permute-start | bytes 786440 | tf_op jit(solution)/shard_map/ppermute | solution.py:129
  76.3 1.3 %collective-permute-start.3 = (bf16[128,1024]{1,0:T(8,128)(2,1)S(1)}, bf16[128,1024]{1,0:T(8,128)(2,1)}, u32[]{:S(2)}, u32[]{:S(2)}) collective-permute-start(bf16[128,1024]{1,0:T(8,128)(2,1)S(1)} %add_add_fusion.1), channel_id=1, source_target_pairs={{0,9},{8,11},{2,4},{6,12},{16,25},{24,27},{18,20},{22,28},{32,41},... | collective-permute-start | bytes 786440 | tf_op jit(solution)/shard_map/ppermute | solution.py:129
  77.6 6.9 %all-to-all-done.1 = bf16[8,2,16,1024]{3,2,1,0:T(8,128)(2,1)S(1)} async-done(((bf16[8,2,16,1024]{3,2,1,0:T(8,128)(2,1)}), bf16[8,2,16,1024]{3,2,1,0:T(8,128)(2,1)S(1)}, u32[]{:S(2)}, u32[]{:S(2)}) %all-to-all-start.1) | async-done | bytes 524320 | tf_op jit(solution)/shard_map/all_to_all | solution.py:108
  84.5 1.9 %collective-permute-start.9 = (bf16[256,1024]{1,0:T(8,128)(2,1)S(1)}, bf16[256,1024]{1,0:T(8,128)(2,1)S(1)}, u32[]{:S(2)}, u32[]{:S(2)}) collective-permute-start(bf16[256,1024]{1,0:T(8,128)(2,1)S(1)} %bitcast.29), channel_id=1, source_target_pairs={{0,16},{16,0},{32,48},{48,32},{1,17},{17,1},{33,49},{49,33},{2,18}... | collective-permute-start | bytes 1572872 | tf_op jit(solution)/shard_map/ppermute | solution.py:117
  86.4 0.1 slice_bitcast_fusion.1
  86.6 6.9 %collective-permute-done.3 = bf16[128,1024]{1,0:T(8,128)(2,1)} collective-permute-done((bf16[128,1024]{1,0:T(8,128)(2,1)S(1)}, bf16[128,1024]{1,0:T(8,128)(2,1)}, u32[]{:S(2)}, u32[]{:S(2)}) %collective-permute-start.3) | collective-permute-done | bytes 262176 | tf_op jit(solution)/shard_map/ppermute | solution.py:129
  93.5 1.1 %add_add_fusion = bf16[128,1024]{1,0:T(8,128)(2,1)S(1)} fusion(bf16[128,1024]{1,0:T(8,128)(2,1)S(1)} %collective-permute-done.5, bf16[128,1024]{1,0:T(8,128)(2,1)} %collective-permute-done.4, bf16[128,1024]{1,0:T(8,128)(2,1)S(1)} %add_add_fusion.1, bf16[128,1024]{1,0:T(8,128)(2,1)} %collective-permute-done.3), kind=kLoop, calls=%fused_computation.48 | loop fusion | flops 393216 | bytes 1310720 | tf_op jit(solution)/shard_map/add | solution.py:130
  94.6 0.1 slice_negate_fusion.2
  94.7 1.3 %reduce-precision_convert_fusion = (bf16[512,1024]{1,0:T(8,128)(2,1)S(1)}, bf16[512,1024]{1,0:T(8,128)(2,1)S(1)}) fusion(bf16[512,512]{1,0:T(8,128)(2,1)S(1)} %get-tuple-element.18, bf16[512,512]{1,0:T(8,128)(2,1)S(1)} %get-tuple-element.17, bf16[256,1024]{1,0:T(8,128)(2,1)S(1)} %collective-permute-done.9, bf16[256,1024]{1,0:T(8,128)(2,1)S(1)} %bitcast.31, ...), kind=kOutput, calls=%fused_computation.13 | convolution fusion | flops 1086324736 | bytes 5242880 | tf_op jit(solution)/shard_map/dot_general | solution.py:112
  96.0 0.1 slice_negate_fusion
  96.1 0.8 fusion.26
  96.9 0.8 maximum_bitcast_fusion
  (24 shorter events, 0.3 us)
Async XLA Ops:
  6.5 64.1 %reduce-scatter.2.cloned.1.call-start = ((), (), s32[]{:S(2)}) async-start(), calls=%async_computation.3 | async-start | bytes 2359296 | tf_op jit(solution)/shard_map/reduce_scatter | solution.py:150
  6.5 7.6 %copy-start.2 = (s32[512]{0:T(512)S(1)}, s32[512]{0:T(512)}, u32[]{:S(2)}) copy-start(s32[512]{0:T(512)} %param.12) | copy-start | bytes 6148
  17.0 52.7 %copy-start = (bf16[2,512,512]{2,1,0:T(8,128)(2,1)S(1)}, bf16[2,512,512]{2,1,0:T(8,128)(2,1)}, u32[]{:S(2)}) copy-start(bf16[2,512,512]{2,1,0:T(8,128)(2,1)} %param.13) | copy-start | bytes 3145732
  17.1 3.9 %collective-permute-start.6 = (bf16[256,1024]{1,0:T(8,128)(2,1)S(1)}, bf16[256,1024]{1,0:T(8,128)(2,1)S(1)}, u32[]{:S(2)}, u32[]{:S(2)}) collective-permute-start(bf16[256,1024]{1,0:T(8,128)(2,1)S(1)} %dynamic-slice_bitcast_fusion), channel_id=1, source_target_pairs={{0,16},{16,0},{32,48},{48,32},{1,17},{17,1},{33,49},{49,33},{2,18}... | collective-permute-start | bytes 1572872 | tf_op jit(solution)/shard_map/ppermute | solution.py:117
  21.1 11.7 %collective-permute-start.7 = (bf16[8,16,1024]{2,1,0:T(8,128)(2,1)S(1)}, bf16[8,16,1024]{2,1,0:T(8,128)(2,1)S(1)}, u32[]{:S(2)}, u32[]{:S(2)}) collective-permute-start(bf16[8,16,1024]{2,1,0:T(8,128)(2,1)S(1)} %dynamic-slice_bitcast_fusion.1), channel_id=1, source_target_pairs={{0,32},{16,48},{32,0},{48,16},{1,33},{17,49},{33,1},{49,17},{2,34}... | collective-permute-start | bytes 786440 | tf_op jit(solution)/shard_map/ppermute | solution.py:117
  58.1 7.3 %collective-permute-start.8 = (bf16[16,1024]{1,0:T(8,128)(2,1)S(1)}, bf16[16,1024]{1,0:T(8,128)(2,1)S(1)}, u32[]{:S(2)}, u32[]{:S(2)}) collective-permute-start(bf16[16,1024]{1,0:T(8,128)(2,1)S(1)} %reduce_sum.12), channel_id=1, source_target_pairs={{0,32},{16,48},{32,0},{48,16},{1,33},{17,49},{33,1},{49,17},{2,34}... | collective-permute-start | bytes 98312 | tf_op jit(solution)/shard_map/ppermute | solution.py:117
  66.2 18.3 %all-to-all-start.1 = ((bf16[8,2,16,1024]{3,2,1,0:T(8,128)(2,1)}), bf16[8,2,16,1024]{3,2,1,0:T(8,128)(2,1)S(1)}, u32[]{:S(2)}, u32[]{:S(2)}) async-start(bf16[8,2,16,1024]{3,2,1,0:T(8,128)(2,1)} %broadcast_in_dim.5), calls=%async_computation.2 | async-start | bytes 1048576 | tf_op jit(solution)/shard_map/all_to_all | solution.py:108
  70.6 3.6 %copy-start.1 = (bf16[128,1024]{1,0:T(8,128)(2,1)S(1)}, bf16[128,1024]{1,0:T(8,128)(2,1)}, u32[]{:S(2)}) copy-start(bf16[128,1024]{1,0:T(8,128)(2,1)} %reduce-scatter.2.cloned.1.call-done) | copy-start | bytes 786436
  70.7 3.5 %collective-permute-start.1 = (bf16[128,1024]{1,0:T(8,128)(2,1)S(1)}, bf16[128,1024]{1,0:T(8,128)(2,1)S(1)}, u32[]{:S(2)}, u32[]{:S(2)}) collective-permute-start(bf16[128,1024]{1,0:T(8,128)(2,1)S(1)} %broadcast_select_fusion), channel_id=1, source_target_pairs={{0,2},{16,18},{32,34},{48,50},{64,66},{80,82},{96,98},{112,114},{1... | collective-permute-start | bytes 786440 | tf_op jit(solution)/shard_map/ppermute | solution.py:129
  71.5 2.7 %collective-permute-start.2 = (bf16[128,1024]{1,0:T(8,128)(2,1)S(1)}, bf16[128,1024]{1,0:T(8,128)(2,1)S(1)}, u32[]{:S(2)}, u32[]{:S(2)}) collective-permute-start(bf16[128,1024]{1,0:T(8,128)(2,1)S(1)} %broadcast_select_fusion), channel_id=1, source_target_pairs={{0,6},{16,22},{32,38},{48,54},{64,70},{80,86},{96,102},{112,118},{... | collective-permute-start | bytes 786440 | tf_op jit(solution)/shard_map/ppermute | solution.py:129
  72.2 2.0 %collective-permute-start = (bf16[128,1024]{1,0:T(8,128)(2,1)S(1)}, bf16[128,1024]{1,0:T(8,128)(2,1)S(1)}, u32[]{:S(2)}, u32[]{:S(2)}) collective-permute-start(bf16[128,1024]{1,0:T(8,128)(2,1)S(1)} %broadcast_select_fusion), channel_id=1, source_target_pairs={{0,8},{16,24},{32,40},{48,56},{64,72},{80,88},{96,104},{112,120},{... | collective-permute-start | bytes 786440 | tf_op jit(solution)/shard_map/ppermute | solution.py:129
  74.3 12.3 %collective-permute-start.5 = (bf16[128,1024]{1,0:T(8,128)(2,1)S(1)}, bf16[128,1024]{1,0:T(8,128)(2,1)S(1)}, u32[]{:S(2)}, u32[]{:S(2)}) collective-permute-start(bf16[128,1024]{1,0:T(8,128)(2,1)S(1)} %add_add_fusion.1), channel_id=1, source_target_pairs={{0,1},{8,15},{2,3},{6,5},{16,17},{24,31},{18,19},{22,21},{32,33},{... | collective-permute-start | bytes 786440 | tf_op jit(solution)/shard_map/ppermute | solution.py:129
  74.9 11.6 %collective-permute-start.4 = (bf16[128,1024]{1,0:T(8,128)(2,1)S(1)}, bf16[128,1024]{1,0:T(8,128)(2,1)}, u32[]{:S(2)}, u32[]{:S(2)}) collective-permute-start(bf16[128,1024]{1,0:T(8,128)(2,1)S(1)} %add_add_fusion.1), channel_id=1, source_target_pairs={{0,7},{8,13},{2,10},{6,14},{16,23},{24,29},{18,26},{22,30},{32,39}... | collective-permute-start | bytes 786440 | tf_op jit(solution)/shard_map/ppermute | solution.py:129
  76.3 17.2 %collective-permute-start.3 = (bf16[128,1024]{1,0:T(8,128)(2,1)S(1)}, bf16[128,1024]{1,0:T(8,128)(2,1)}, u32[]{:S(2)}, u32[]{:S(2)}) collective-permute-start(bf16[128,1024]{1,0:T(8,128)(2,1)S(1)} %add_add_fusion.1), channel_id=1, source_target_pairs={{0,9},{8,11},{2,4},{6,12},{16,25},{24,27},{18,20},{22,28},{32,41},... | collective-permute-start | bytes 786440 | tf_op jit(solution)/shard_map/ppermute | solution.py:129
  84.5 10.1 %collective-permute-start.9 = (bf16[256,1024]{1,0:T(8,128)(2,1)S(1)}, bf16[256,1024]{1,0:T(8,128)(2,1)S(1)}, u32[]{:S(2)}, u32[]{:S(2)}) collective-permute-start(bf16[256,1024]{1,0:T(8,128)(2,1)S(1)} %bitcast.29), channel_id=1, source_target_pairs={{0,16},{16,0},{32,48},{48,32},{1,17},{17,1},{33,49},{49,33},{2,18}... | collective-permute-start | bytes 1572872 | tf_op jit(solution)/shard_map/ppermute | solution.py:117
Sparse Core Ops, SparseCore 0:
  14.2 53.8 reduce-scatter.1

commit v4 on v3

--- a/solution.py
+++ b/solution.py
@@ -15,8 +15,8 @@
 
 
 def terms_kernel(
-    green_ref, weight_ref, index_ref, left_hbm, right_hbm, terms_hbm,
-    left_ref, right_ref, stack_ref, terms_ref, in_sems, out_sems,
+    green_ref, weight_ref, index_ref, pivot_ref, left_hbm, right_hbm, terms_hbm, send_hbm, keep_hbm,
+    left_ref, right_ref, stack_ref, terms_ref, picked_ref, in_sems, out_sems, picked_sems,
 ):
     points, width = right_ref.shape[1], right_ref.shape[2]
     right_copy = pltpu.make_async_copy(right_hbm, right_ref, in_sems.at[0])
@@ -65,32 +65,56 @@
         )
         copy.start()
         copies.append(copy)
+
+    grid_row = lax.axis_index("row")
+    core = grid_row % 2
+    tile_rows = terms_ref.shape[0]
+    pivot_groups = pivot_ref.shape[0]
+    pivot_fill = jnp.zeros((-pivot_groups % SUBLANES, LANES), jnp.int32)
+    local = jnp.transpose(jnp.concatenate([pivot_ref[...] - grid_row * tile_rows, pivot_fill], axis=0))
+    row_index = lax.broadcasted_iota(jnp.int32, (LANES, tile_rows), 1)
+    side = pivot_groups // 2
+    for part, picked_hbm in enumerate((send_hbm, keep_hbm)):
+        for group in range(side):
+            low, high = local[:, group : group + 1], local[:, side + group : side + group + 1]
+            wanted = jnp.where(core == (1 - part), low, high)
+            chosen = jnp.where(row_index == wanted, 1.0, 0.0).astype(BF16)
+            rows = slice(group * LANES, (group + 1) * LANES)
+            picked = jnp.dot(chosen, terms_ref[...], preferred_element_type=F32)
+            picked_ref[part, rows, :] = picked.astype(BF16)
+        copy = pltpu.make_async_copy(picked_ref.at[part], picked_hbm, picked_sems.at[part])
+        copy.start()
+        copies.append(copy)
     for copy in copies:
         copy.wait()
 
 
-def partial_terms(left_basis, right_basis, point_weight, shell_index, green_table):
+def partial_terms(left_basis, right_basis, point_weight, shell_index, green_table, pivot_rows):
     _, tile_rows, points = left_basis.shape
     width = right_basis.shape[2]
     groups = points // LANES
+    pivots_count = pivot_rows.shape[0]
     in_vmem = pl.BlockSpec(memory_space=pltpu.VMEM)
     in_hbm = pl.BlockSpec(memory_space=pltpu.HBM)
     return pl.pallas_call(
         terms_kernel,
-        in_specs=[pl.BlockSpec(memory_space=pltpu.SMEM), in_vmem, in_vmem, in_hbm, in_hbm],
-        out_specs=in_hbm,
-        out_shape=jax.ShapeDtypeStruct((tile_rows, 2 * width), BF16),
+        in_specs=[pl.BlockSpec(memory_space=pltpu.SMEM), in_vmem, in_vmem, in_vmem, in_hbm, in_hbm],
+        out_specs=[in_hbm] * 3,
+        out_shape=[jax.ShapeDtypeStruct((tile_rows, 2 * width), BF16)]
+        + [jax.ShapeDtypeStruct((pivots_count // 2, 2 * width), BF16)] * 2,
         scratch_shapes=[
             pltpu.VMEM(left_basis.shape, BF16),
             pltpu.VMEM(right_basis.shape, BF16),
             pltpu.VMEM((2 * points, 2 * width), BF16),
             pltpu.VMEM((tile_rows, 2 * width), BF16),
+            pltpu.VMEM((2, pivots_count // 2, 2 * width), BF16),
             pltpu.SemaphoreType.DMA((2,)),
             pltpu.SemaphoreType.DMA((ROW_STEPS,)),
+            pltpu.SemaphoreType.DMA((2,)),
         ],
         compiler_params=pltpu.CompilerParams(vmem_limit_bytes=62 * 1024 * 1024),
         cost_estimate=pl.CostEstimate(
-            flops=8 * tile_rows * points * width,
+            flops=8 * tile_rows * points * width + 4 * pivots_count * tile_rows * width,
             transcendentals=0,
             bytes_accessed=2 * (left_basis.size + right_basis.size + 2 * tile_rows * width),
         ),
@@ -99,6 +123,7 @@
         green_table.T,
         point_weight.reshape(groups, LANES),
         shell_index.reshape(groups, LANES),
+        pivot_rows.reshape(pivots_count // LANES, LANES),
         left_basis,
         right_basis,
     )
@@ -146,14 +171,12 @@
     pivots_count = pivot_rows.shape[0]
     grid_row = lax.axis_index("row")
     core, chip = grid_row % 2, grid_row // 2
-    terms = partial_terms(left_basis, right_basis, point_weight, shell_index, green_table)
+    terms, passed, kept = partial_terms(
+        left_basis, right_basis, point_weight, shell_index, green_table, pivot_rows
+    )
     tile_sums = lax.psum_scatter(terms, "shell", scatter_dimension=0, tiled=True)
 
-    tile_index = lax.broadcasted_iota(jnp.int32, (pivots_count, tile_rows), 1) + grid_row * tile_rows
-    chosen = (pivot_rows[:, None] == tile_index).astype(BF16)
-    picked = dot(chosen, terms).astype(BF16)
-    picked = picked.reshape(2, pivots_count // 2, 2 * width)
-    picked = pick(picked, core, 0) + swap(pick(picked, 1 - core, 0), 1)
+    picked = kept + swap(passed, 1)
     share_rows = pivots_count // (4 * shells)
     picked = picked.reshape(shells, 2, share_rows, 2 * width)
     picked = pick(picked, chip, 1) + swap(pick(picked, 1 - chip, 1), 2)
@@ -161,8 +184,8 @@
     share = jnp.sum(shares.astype(F32), axis=0).astype(BF16)
     pair = ordered(share, swap(share, 2), chip)
     half = exchange(jnp.broadcast_to(pair[None], (shells,) + pair.shape), "shell").reshape(pivots_count // 2, 2 * width)
-    panel = jnp.where(lax.axis_index("col") == 0, tile_sums, jnp.zeros_like(tile_sums))
-    panel = forward(panel, FIRST_SENDS)
+    first = [lax.ppermute(tile_sums, "col", pairs) for pairs in FIRST_SENDS]
+    panel = jnp.where(lax.axis_index("col") == 0, tile_sums, first[0] + first[1] + first[2])
     half, _ = lax.optimization_barrier((half, panel))
     panel = forward(panel, SECOND_SENDS)
     pivots = jnp.concatenate([half, swap(half, 1)], axis=0)

time: 105 us -> 105 us (level)
  matrix products: 4.91 us -> 2.04 us
  waiting for transfers between devices: 28 us -> 30.2 us
  Pallas kernels: 7.5 us -> 8.65 us
    dot_general x3 -> x2, matrix products: 4.91 us -> 2.04 us  [dot(): return jnp.dot(a, b, preferred_element_type=F32)]
    ppermute x6 -> x3, starting transfers between devices: 5.5 us -> 2.65 us  [forward(): arrived = [lax.ppermute(value, 'col', pairs) for pairs in sends]]
    ppermute x0 -> x3, starting transfers between devices: none -> 2.15 us  [body(): first = [lax.ppermute(tile_sums, 'col', pairs) for pairs in FIRST_SENDS]]
    ppermute x6 -> x3, waiting for transfers between devices: 6.93 us -> 8.44 us  [forward(): arrived = [lax.ppermute(value, 'col', pairs) for pairs in sends]]
    add x2 -> x1, other arithmetic: 0.06 us -> 1.23 us  [body(): picked = kept + swap(passed, 1)]
    pallas_call x1, Pallas kernels: 7.5 us -> 8.65 us  [partial_terms(): pl.pallas_call(terms_kernel, in_specs=[pl.BlockSpec(memory_space=pltpu.SM...]
    add x2 -> x1, other arithmetic: 1.14 us -> 0.05 us  [forward(): return value + arrived[0] + arrived[1] + arrived[2]]
  transfers between devices with their start and end apart: 12 -> 12, of which waited for: 5 -> 5; matrix products, arithmetic and copies ran while one was open for 7% -> 4% of each run, Pallas kernels for 0% -> 0%
where the time goes in v4:
time: 105 us; the launch traced here: 104 us
  waiting for transfers between devices  30.2 us (29%)
  blocking collectives  25 us (24%)
  starting transfers between devices  19 us (18%)
  between operations  13.7 us (13%)
  Pallas kernels  8.65 us (8%)
  other arithmetic  3.78 us (4%)
  matrix products  2.04 us (2%)
  local copies, waits for them, and re-layouts  1.94 us (2%)
    all_to_all x1, blocking collectives, exchange(): return lax.all_to_all(blocks, axes, 0, 0, tiled=False)  25 us
    ppermute x4, waiting for transfers between devices, swap(): return lax.ppermute(block, 'row', [(i, i ^ bit) for i in range(count)])  14.3 us
    ppermute x4, starting transfers between devices, swap(): return lax.ppermute(block, 'row', [(i, i ^ bit) for i in range(count)])  10.7 us
    pallas_call x1, Pallas kernels, partial_terms(): pl.pallas_call(terms_kernel, in_specs=[pl.BlockSpec(memory_space=pltpu.SM...  8.65 us
    ppermute x3, waiting for transfers between devices, forward(): arrived = [lax.ppermute(value, 'col', pairs) for pairs in sends]  8.44 us
    all_to_all x1, waiting for transfers between devices, exchange(): return lax.all_to_all(blocks, axes, 0, 0, tiled=False)  7.43 us
    all_to_all x1, starting transfers between devices, exchange(): return lax.all_to_all(blocks, axes, 0, 0, tiled=False)  3.5 us
    ppermute x3, starting transfers between devices, forward(): arrived = [lax.ppermute(value, 'col', pairs) for pairs in sends]  2.65 us
  transfers between devices with their start and end apart: 12, of which 5 were waited for; matrix products, arithmetic and copies ran while one was open for 4% of the time, Pallas kernels for 0%

profile of v4, /device:TPU:14, one launch (start us, length us, event | category | flops | bytes accessed | tf_op | source)
XLA Modules:
  0.0 104.4 jit_solution(17288937353672994719)
XLA Ops:
  6.5 8.6 %terms.1 = (bf16[1024,1024]{1,0:T(8,128)(2,1)}, bf16[256,1024]{1,0:T(8,128)(2,1)}, bf16[256,1024]{1,0:T(8,128)(2,1)}) custom-call(f32[2,12]{1,0:T(2,128)} %bitcast.34, f32[6,128]{1,0:T(8,128)} %bitcast.31, s32[6,128]{1,0:T(8,128)} %bitcast.32, s32[4,128]{1,0:T(4,128)} %bitcast.33, bf16[2,1024,768]{2,1,0:T(8,128)(2,1)} %left_hbm.1, bf16[2,768,512]{2,1,0:T(8,128)(2,1)} %right_hbm.1), custom_call_target="tpu_custom_call" | custom-call | flops 4294967296 | bytes 6815744 | tf_op jit(solution)/shard_map/terms/pallas_call | solution.py:99
  15.2 0.0 reduce-scatter.2.cloned.1.call-update
  15.2 0.0 copy-start
  15.2 2.1 %collective-permute-start.6 = (bf16[256,1024]{1,0:T(8,128)(2,1)}, bf16[256,1024]{1,0:T(8,128)(2,1)S(1)}, u32[]{:S(2)}, u32[]{:S(2)}) collective-permute-start(bf16[256,1024]{1,0:T(8,128)(2,1)} %get-tuple-element.11), channel_id=1, source_target_pairs={{0,16},{16,0},{32,48},{48,32},{1,17},{17,1},{33,49},{49,33},{2,18}... | collective-permute-start | bytes 1572872 | tf_op jit(solution)/shard_map/ppermute | solution.py:142
  17.3 2.1 %collective-permute-done.6 = bf16[256,1024]{1,0:T(8,128)(2,1)S(1)} collective-permute-done((bf16[256,1024]{1,0:T(8,128)(2,1)}, bf16[256,1024]{1,0:T(8,128)(2,1)S(1)}, u32[]{:S(2)}, u32[]{:S(2)}) %collective-permute-start.6) | collective-permute-done | bytes 524320 | tf_op jit(solution)/shard_map/ppermute | solution.py:142
  19.4 1.2 %add.42 = bf16[256,1024]{1,0:T(8,128)(2,1)S(1)} add(bf16[256,1024]{1,0:T(8,128)(2,1)} %get-tuple-element.10, bf16[256,1024]{1,0:T(8,128)(2,1)S(1)} %collective-permute-done.6) | non-fusion elementwise | flops 262144 | bytes 1572864 | tf_op jit(solution)/shard_map/add | solution.py:179
  20.6 3.3 %collective-permute-start.7 = (bf16[8,16,1024]{2,1,0:T(8,128)(2,1)S(1)}, bf16[8,16,1024]{2,1,0:T(8,128)(2,1)S(1)}, u32[]{:S(2)}, u32[]{:S(2)}) collective-permute-start(bf16[8,16,1024]{2,1,0:T(8,128)(2,1)S(1)} %dynamic-slice_bitcast_fusion), channel_id=1, source_target_pairs={{0,32},{16,48},{32,0},{48,16},{1,33},{17,49},{33,1},{49,17},{2,34}... | collective-permute-start | bytes 786440 | tf_op jit(solution)/shard_map/ppermute | solution.py:142
  24.0 8.4 %collective-permute-done.7 = bf16[8,16,1024]{2,1,0:T(8,128)(2,1)S(1)} collective-permute-done((bf16[8,16,1024]{2,1,0:T(8,128)(2,1)S(1)}, bf16[8,16,1024]{2,1,0:T(8,128)(2,1)S(1)}, u32[]{:S(2)}, u32[]{:S(2)}) %collective-permute-start.7) | collective-permute-done | bytes 262176 | tf_op jit(solution)/shard_map/ppermute | solution.py:142
  32.4 25.0 %all_to_all.10 = bf16[8,16,1024]{2,1,0:T(8,128)(2,1)S(1)} all-to-all(bf16[8,16,1024]{2,1,0:T(8,128)(2,1)S(1)} %bitcast_add_fusion), channel_id=1, replica_groups=mesh['shell'=8,'row'=4,'col'=16] {'shell'}, dimensions={0} | all-to-all | bytes 524288 | tf_op jit(solution)/shard_map/all_to_all | solution.py:133
  57.5 3.4 %collective-permute-start.8 = (bf16[16,1024]{1,0:T(8,128)(2,1)S(1)}, bf16[16,1024]{1,0:T(8,128)(2,1)S(1)}, u32[]{:S(2)}, u32[]{:S(2)}) collective-permute-start(bf16[16,1024]{1,0:T(8,128)(2,1)S(1)} %reduce_sum.12), channel_id=1, source_target_pairs={{0,32},{16,48},{32,0},{48,16},{1,33},{17,49},{33,1},{49,17},{2,34}... | collective-permute-start | bytes 98312 | tf_op jit(solution)/shard_map/ppermute | solution.py:142
  61.0 3.9 %collective-permute-done.8 = bf16[16,1024]{1,0:T(8,128)(2,1)S(1)} collective-permute-done((bf16[16,1024]{1,0:T(8,128)(2,1)S(1)}, bf16[16,1024]{1,0:T(8,128)(2,1)S(1)}, u32[]{:S(2)}, u32[]{:S(2)}) %collective-permute-start.8) | collective-permute-done | bytes 32800 | tf_op jit(solution)/shard_map/ppermute | solution.py:142
  64.8 0.9 broadcast_in_dim.2
  65.7 3.5 %all-to-all-start.1 = ((bf16[8,2,16,1024]{3,2,1,0:T(8,128)(2,1)}), bf16[8,2,16,1024]{3,2,1,0:T(8,128)(2,1)S(1)}, u32[]{:S(2)}, u32[]{:S(2)}) async-start(bf16[8,2,16,1024]{3,2,1,0:T(8,128)(2,1)} %broadcast_in_dim.2), calls=%async_computation.2 | async-start | bytes 1048576 | tf_op jit(solution)/shard_map/all_to_all | solution.py:133
  69.2 0.9 fusion.32
  70.1 0.8 collective-permute-start.2
  70.9 0.7 collective-permute-start.1
  71.6 0.7 collective-permute-start
  72.3 1.3 %maximum_select_fusion = bf16[2,512,512]{2,1,0:T(8,128)(2,1)S(1)} fusion(bf16[2,512,512]{2,1,0:T(8,128)(2,1)S(1)} %copy-done, bf16[2,512,256]{2,1,0:T(8,128)(2,1)} %get-tuple-element.22, bf16[2,512,256]{2,1,0:T(8,128)(2,1)S(1)} %get-tuple-element.21, pred[]{:T(512)S(6)} %eq.12), kind=kLoop, calls=%fused_computation.24 | loop fusion | flops 2621440 | bytes 3145729 | tf_op jit(solution)/shard_map/jit(_where)/select_n | solution.py:195
  73.6 0.1 add_select_fusion
  73.7 0.7 collective-permute-start.5
  74.4 0.7 collective-permute-start.4
  75.1 1.3 %collective-permute-start.3 = (bf16[128,1024]{1,0:T(8,128)(2,1)S(1)}, bf16[128,1024]{1,0:T(8,128)(2,1)S(1)}, u32[]{:S(2)}, u32[]{:S(2)}) collective-permute-start(bf16[128,1024]{1,0:T(8,128)(2,1)S(1)} %add_select_fusion), channel_id=1, source_target_pairs={{0,9},{8,11},{2,4},{6,12},{16,25},{24,27},{18,20},{22,28},{32,41},... | collective-permute-start | bytes 786440 | tf_op jit(solution)/shard_map/ppermute | solution.py:154
  76.4 7.4 %all-to-all-done.1 = bf16[8,2,16,1024]{3,2,1,0:T(8,128)(2,1)S(1)} async-done(((bf16[8,2,16,1024]{3,2,1,0:T(8,128)(2,1)}), bf16[8,2,16,1024]{3,2,1,0:T(8,128)(2,1)S(1)}, u32[]{:S(2)}, u32[]{:S(2)}) %all-to-all-start.1) | async-done | bytes 524320 | tf_op jit(solution)/shard_map/all_to_all | solution.py:133
  83.8 1.9 %collective-permute-start.9 = (bf16[256,1024]{1,0:T(8,128)(2,1)S(1)}, bf16[256,1024]{1,0:T(8,128)(2,1)S(1)}, u32[]{:S(2)}, u32[]{:S(2)}) collective-permute-start(bf16[256,1024]{1,0:T(8,128)(2,1)S(1)} %bitcast.26), channel_id=1, source_target_pairs={{0,16},{16,0},{32,48},{48,32},{1,17},{17,1},{33,49},{49,33},{2,18}... | collective-permute-start | bytes 1572872 | tf_op jit(solution)/shard_map/ppermute | solution.py:142
  85.7 0.1 slice_bitcast_fusion.1
  85.9 8.4 %collective-permute-done.3 = bf16[128,1024]{1,0:T(8,128)(2,1)S(1)} collective-permute-done((bf16[128,1024]{1,0:T(8,128)(2,1)S(1)}, bf16[128,1024]{1,0:T(8,128)(2,1)S(1)}, u32[]{:S(2)}, u32[]{:S(2)}) %collective-permute-start.3) | collective-permute-done | bytes 262176 | tf_op jit(solution)/shard_map/ppermute | solution.py:154
  94.3 0.1 add_add_fusion
  94.4 0.1 slice_negate_fusion.2
  94.5 1.3 %reduce-precision_convert_fusion = (bf16[512,1024]{1,0:T(8,128)(2,1)S(1)}, bf16[512,1024]{1,0:T(8,128)(2,1)S(1)}) fusion(bf16[512,512]{1,0:T(8,128)(2,1)S(1)} %get-tuple-element.24, bf16[512,512]{1,0:T(8,128)(2,1)S(1)} %get-tuple-element.23, bf16[256,1024]{1,0:T(8,128)(2,1)S(1)} %collective-permute-done.9, bf16[256,1024]{1,0:T(8,128)(2,1)S(1)} %bitcast.28, ...), kind=kOutput, calls=%fused_computation.13 | convolution fusion | flops 1086324736 | bytes 5242880 | tf_op jit(solution)/shard_map/dot_general | solution.py:137
  95.8 0.1 slice_negate_fusion
  95.9 0.8 fusion.21
  96.7 0.8 maximum_bitcast_fusion
  (18 shorter events, 0.2 us)
Async XLA Ops:
  6.5 63.6 %reduce-scatter.2.cloned.1.call-start = ((), (), s32[]{:S(2)}) async-start(), calls=%async_computation.3 | async-start | bytes 2359296 | tf_op jit(solution)/shard_map/reduce_scatter | solution.py:177
  15.2 54.0 %copy-start = (bf16[2,512,512]{2,1,0:T(8,128)(2,1)S(1)}, bf16[2,512,512]{2,1,0:T(8,128)(2,1)}, u32[]{:S(2)}) copy-start(bf16[2,512,512]{2,1,0:T(8,128)(2,1)} %param.13) | copy-start | bytes 3145732
  15.2 4.1 %collective-permute-start.6 = (bf16[256,1024]{1,0:T(8,128)(2,1)}, bf16[256,1024]{1,0:T(8,128)(2,1)S(1)}, u32[]{:S(2)}, u32[]{:S(2)}) collective-permute-start(bf16[256,1024]{1,0:T(8,128)(2,1)} %get-tuple-element.11), channel_id=1, source_target_pairs={{0,16},{16,0},{32,48},{48,32},{1,17},{17,1},{33,49},{49,33},{2,18}... | collective-permute-start | bytes 1572872 | tf_op jit(solution)/shard_map/ppermute | solution.py:142
  20.6 11.7 %collective-permute-start.7 = (bf16[8,16,1024]{2,1,0:T(8,128)(2,1)S(1)}, bf16[8,16,1024]{2,1,0:T(8,128)(2,1)S(1)}, u32[]{:S(2)}, u32[]{:S(2)}) collective-permute-start(bf16[8,16,1024]{2,1,0:T(8,128)(2,1)S(1)} %dynamic-slice_bitcast_fusion), channel_id=1, source_target_pairs={{0,32},{16,48},{32,0},{48,16},{1,33},{17,49},{33,1},{49,17},{2,34}... | collective-permute-start | bytes 786440 | tf_op jit(solution)/shard_map/ppermute | solution.py:142
  57.5 7.3 %collective-permute-start.8 = (bf16[16,1024]{1,0:T(8,128)(2,1)S(1)}, bf16[16,1024]{1,0:T(8,128)(2,1)S(1)}, u32[]{:S(2)}, u32[]{:S(2)}) collective-permute-start(bf16[16,1024]{1,0:T(8,128)(2,1)S(1)} %reduce_sum.12), channel_id=1, source_target_pairs={{0,32},{16,48},{32,0},{48,16},{1,33},{17,49},{33,1},{49,17},{2,34}... | collective-permute-start | bytes 98312 | tf_op jit(solution)/shard_map/ppermute | solution.py:142
  65.7 18.1 %all-to-all-start.1 = ((bf16[8,2,16,1024]{3,2,1,0:T(8,128)(2,1)}), bf16[8,2,16,1024]{3,2,1,0:T(8,128)(2,1)S(1)}, u32[]{:S(2)}, u32[]{:S(2)}) async-start(bf16[8,2,16,1024]{3,2,1,0:T(8,128)(2,1)} %broadcast_in_dim.2), calls=%async_computation.2 | async-start | bytes 1048576 | tf_op jit(solution)/shard_map/all_to_all | solution.py:133
  70.1 3.5 %copy-start.1 = (bf16[128,1024]{1,0:T(8,128)(2,1)S(1)}, bf16[128,1024]{1,0:T(8,128)(2,1)}, u32[]{:S(2)}) copy-start(bf16[128,1024]{1,0:T(8,128)(2,1)} %reduce-scatter.2.cloned.1.call-done) | copy-start | bytes 786436
  70.1 3.5 %collective-permute-start.2 = (bf16[128,1024]{1,0:T(8,128)(2,1)}, bf16[128,1024]{1,0:T(8,128)(2,1)S(1)}, u32[]{:S(2)}, u32[]{:S(2)}) collective-permute-start(bf16[128,1024]{1,0:T(8,128)(2,1)} %reduce-scatter.2.cloned.1.call-done), channel_id=1, source_target_pairs={{0,6},{16,22},{32,38},{48,54},{64,70},{80,86},{96,102},{112,118},{... | collective-permute-start | bytes 786440 | tf_op jit(solution)/shard_map/ppermute | solution.py:187
  70.9 2.7 %collective-permute-start.1 = (bf16[128,1024]{1,0:T(8,128)(2,1)}, bf16[128,1024]{1,0:T(8,128)(2,1)S(1)}, u32[]{:S(2)}, u32[]{:S(2)}) collective-permute-start(bf16[128,1024]{1,0:T(8,128)(2,1)} %reduce-scatter.2.cloned.1.call-done), channel_id=1, source_target_pairs={{0,2},{16,18},{32,34},{48,50},{64,66},{80,82},{96,98},{112,114},{1... | collective-permute-start | bytes 786440 | tf_op jit(solution)/shard_map/ppermute | solution.py:187
  71.6 2.0 %collective-permute-start = (bf16[128,1024]{1,0:T(8,128)(2,1)}, bf16[128,1024]{1,0:T(8,128)(2,1)S(1)}, u32[]{:S(2)}, u32[]{:S(2)}) collective-permute-start(bf16[128,1024]{1,0:T(8,128)(2,1)} %reduce-scatter.2.cloned.1.call-done), channel_id=1, source_target_pairs={{0,8},{16,24},{32,40},{48,56},{64,72},{80,88},{96,104},{112,120},{... | collective-permute-start | bytes 786440 | tf_op jit(solution)/shard_map/ppermute | solution.py:187
  73.7 12.1 %collective-permute-start.5 = (bf16[128,1024]{1,0:T(8,128)(2,1)S(1)}, bf16[128,1024]{1,0:T(8,128)(2,1)S(1)}, u32[]{:S(2)}, u32[]{:S(2)}) collective-permute-start(bf16[128,1024]{1,0:T(8,128)(2,1)S(1)} %add_select_fusion), channel_id=1, source_target_pairs={{0,1},{8,15},{2,3},{6,5},{16,17},{24,31},{18,19},{22,21},{32,33},{... | collective-permute-start | bytes 786440 | tf_op jit(solution)/shard_map/ppermute | solution.py:154
  74.4 11.5 %collective-permute-start.4 = (bf16[128,1024]{1,0:T(8,128)(2,1)S(1)}, bf16[128,1024]{1,0:T(8,128)(2,1)S(1)}, u32[]{:S(2)}, u32[]{:S(2)}) collective-permute-start(bf16[128,1024]{1,0:T(8,128)(2,1)S(1)} %add_select_fusion), channel_id=1, source_target_pairs={{0,7},{8,13},{2,10},{6,14},{16,23},{24,29},{18,26},{22,30},{32,39}... | collective-permute-start | bytes 786440 | tf_op jit(solution)/shard_map/ppermute | solution.py:154
  75.1 19.2 %collective-permute-start.3 = (bf16[128,1024]{1,0:T(8,128)(2,1)S(1)}, bf16[128,1024]{1,0:T(8,128)(2,1)S(1)}, u32[]{:S(2)}, u32[]{:S(2)}) collective-permute-start(bf16[128,1024]{1,0:T(8,128)(2,1)S(1)} %add_select_fusion), channel_id=1, source_target_pairs={{0,9},{8,11},{2,4},{6,12},{16,25},{24,27},{18,20},{22,28},{32,41},... | collective-permute-start | bytes 786440 | tf_op jit(solution)/shard_map/ppermute | solution.py:154
  83.8 10.6 %collective-permute-start.9 = (bf16[256,1024]{1,0:T(8,128)(2,1)S(1)}, bf16[256,1024]{1,0:T(8,128)(2,1)S(1)}, u32[]{:S(2)}, u32[]{:S(2)}) collective-permute-start(bf16[256,1024]{1,0:T(8,128)(2,1)S(1)} %bitcast.26), channel_id=1, source_target_pairs={{0,16},{16,0},{32,48},{48,32},{1,17},{17,1},{33,49},{49,33},{2,18}... | collective-permute-start | bytes 1572872 | tf_op jit(solution)/shard_map/ppermute | solution.py:142
Sparse Core Ops, SparseCore 0:
  15.3 54.2 reduce-scatter.1

commit v5 on v4

--- a/solution.py
+++ b/solution.py
@@ -176,10 +176,11 @@
     )
     tile_sums = lax.psum_scatter(terms, "shell", scatter_dimension=0, tiled=True)
 
-    picked = kept + swap(passed, 1)
     share_rows = pivots_count // (4 * shells)
-    picked = picked.reshape(shells, 2, share_rows, 2 * width)
-    picked = pick(picked, chip, 1) + swap(pick(picked, 1 - chip, 1), 2)
+    kept = kept.reshape(shells, 2, share_rows, 2 * width)
+    got = swap(passed, 1).reshape(kept.shape)
+    leaving = pick(kept, 1 - chip, 1) + pick(got, 1 - chip, 1)
+    picked = pick(kept, chip, 1) + pick(got, chip, 1) + swap(leaving, 2)
     shares = exchange(picked, "shell")
     share = jnp.sum(shares.astype(F32), axis=0).astype(BF16)
     pair = ordered(share, swap(share, 2), chip)

time: 105 us -> 107 us (1.019)
  other arithmetic: 3.78 us -> 5.43 us
  transfers between devices with their start and end apart: 12 -> 12, of which waited for: 5 -> 5; matrix products, arithmetic and copies ran while one was open for 4% -> 6% of each run, Pallas kernels for 0% -> 0%
where the time goes in v5:
time: 107 us
  waiting for transfers between devices  30.3 us (28%)
  blocking collectives  25.2 us (24%)
  starting transfers between devices  18.9 us (18%)
  between operations  13.7 us (13%)
  Pallas kernels  8.64 us (8%)
  other arithmetic  5.43 us (5%)
  local copies, waits for them, and re-layouts  2.71 us (3%)
  matrix products  2.03 us (2%)
    all_to_all x1, blocking collectives, exchange(): return lax.all_to_all(blocks, axes, 0, 0, tiled=False)  25.2 us
    ppermute x4, waiting for transfers between devices, swap(): return lax.ppermute(block, 'row', [(i, i ^ bit) for i in range(count)])  14.4 us
    ppermute x4, starting transfers between devices, swap(): return lax.ppermute(block, 'row', [(i, i ^ bit) for i in range(count)])  10.6 us
    pallas_call x1, Pallas kernels, partial_terms(): pl.pallas_call(terms_kernel, in_specs=[pl.BlockSpec(memory_space=pltpu.SM...  8.64 us
    ppermute x3, waiting for transfers between devices, forward(): arrived = [lax.ppermute(value, 'col', pairs) for pairs in sends]  8.12 us
    all_to_all x1, waiting for transfers between devices, exchange(): return lax.all_to_all(blocks, axes, 0, 0, tiled=False)  7.66 us
    all_to_all x1, starting transfers between devices, exchange(): return lax.all_to_all(blocks, axes, 0, 0, tiled=False)  3.5 us
    ppermute x3, starting transfers between devices, forward(): arrived = [lax.ppermute(value, 'col', pairs) for pairs in sends]  2.65 us
  transfers between devices with their start and end apart: 12, of which 5 were waited for; matrix products, arithmetic and copies ran while one was open for 6% of the time, Pallas kernels for 0%

profile of v5, /device:TPU:14, one launch (start us, length us, event | category | flops | bytes accessed | tf_op | source)
XLA Modules:
  0.0 106.8 jit_solution(1695725168007359767)
XLA Ops:
  6.5 8.6 %terms.1 = (bf16[1024,1024]{1,0:T(8,128)(2,1)}, bf16[256,1024]{1,0:T(8,128)(2,1)}, bf16[256,1024]{1,0:T(8,128)(2,1)}) custom-call(f32[2,12]{1,0:T(2,128)} %bitcast.47, f32[6,128]{1,0:T(8,128)} %bitcast.44, s32[6,128]{1,0:T(8,128)} %bitcast.45, s32[4,128]{1,0:T(4,128)} %bitcast.46, bf16[2,1024,768]{2,1,0:T(8,128)(2,1)} %left_hbm.1, bf16[2,768,512]{2,1,0:T(8,128)(2,1)} %right_hbm.1), custom_call_target="tpu_custom_call" | custom-call | flops 4294967296 | bytes 6815744 | tf_op jit(solution)/shard_map/terms/pallas_call | solution.py:99
  15.2 2.1 %collective-permute-start.6 = (bf16[256,1024]{1,0:T(8,128)(2,1)}, bf16[256,1024]{1,0:T(8,128)(2,1)S(1)}, u32[]{:S(2)}, u32[]{:S(2)}) collective-permute-start(bf16[256,1024]{1,0:T(8,128)(2,1)} %get-tuple-element.11), channel_id=1, source_target_pairs={{0,16},{16,0},{32,48},{48,32},{1,17},{17,1},{33,49},{49,33},{2,18}... | collective-permute-start | bytes 1572872 | tf_op jit(solution)/shard_map/ppermute | solution.py:142
  17.3 2.1 %collective-permute-done.6 = bf16[256,1024]{1,0:T(8,128)(2,1)S(1)} collective-permute-done((bf16[256,1024]{1,0:T(8,128)(2,1)}, bf16[256,1024]{1,0:T(8,128)(2,1)S(1)}, u32[]{:S(2)}, u32[]{:S(2)}) %collective-permute-start.6) | collective-permute-done | bytes 524320 | tf_op jit(solution)/shard_map/ppermute | solution.py:142
  19.4 1.0 add_bitcast_fusion
  20.4 3.3 %collective-permute-start.7 = (bf16[8,16,1024]{2,1,0:T(8,128)(2,1)S(1)}, bf16[8,16,1024]{2,1,0:T(8,128)(2,1)S(1)}, u32[]{:S(2)}, u32[]{:S(2)}) collective-permute-start(bf16[8,16,1024]{2,1,0:T(8,128)(2,1)S(1)} %add_bitcast_fusion), channel_id=1, source_target_pairs={{0,32},{16,48},{32,0},{48,16},{1,33},{17,49},{33,1},{49,17},{2,34}... | collective-permute-start | bytes 786440 | tf_op jit(solution)/shard_map/ppermute | solution.py:142
  23.7 8.4 %collective-permute-done.7 = bf16[8,16,1024]{2,1,0:T(8,128)(2,1)S(1)} collective-permute-done((bf16[8,16,1024]{2,1,0:T(8,128)(2,1)S(1)}, bf16[8,16,1024]{2,1,0:T(8,128)(2,1)S(1)}, u32[]{:S(2)}, u32[]{:S(2)}) %collective-permute-start.7) | collective-permute-done | bytes 262176 | tf_op jit(solution)/shard_map/ppermute | solution.py:142
  32.1 1.0 fusion.31
  33.1 25.2 %all_to_all.10 = bf16[8,16,1024]{2,1,0:T(8,128)(2,1)S(1)} all-to-all(bf16[8,16,1024]{2,1,0:T(8,128)(2,1)S(1)} %fusion.31), channel_id=1, replica_groups=mesh['shell'=8,'row'=4,'col'=16] {'shell'}, dimensions={0} | all-to-all | bytes 524288 | tf_op jit(solution)/shard_map/all_to_all | solution.py:133
  58.3 3.3 %collective-permute-start.8 = (bf16[16,1024]{1,0:T(8,128)(2,1)S(1)}, bf16[16,1024]{1,0:T(8,128)(2,1)S(1)}, u32[]{:S(2)}, u32[]{:S(2)}) collective-permute-start(bf16[16,1024]{1,0:T(8,128)(2,1)S(1)} %reduce_sum.12), channel_id=1, source_target_pairs={{0,32},{16,48},{32,0},{48,16},{1,33},{17,49},{33,1},{49,17},{2,34}... | collective-permute-start | bytes 98312 | tf_op jit(solution)/shard_map/ppermute | solution.py:142
  61.6 4.0 %collective-permute-done.8 = bf16[16,1024]{1,0:T(8,128)(2,1)S(1)} collective-permute-done((bf16[16,1024]{1,0:T(8,128)(2,1)S(1)}, bf16[16,1024]{1,0:T(8,128)(2,1)S(1)}, u32[]{:S(2)}, u32[]{:S(2)}) %collective-permute-start.8) | collective-permute-done | bytes 32800 | tf_op jit(solution)/shard_map/ppermute | solution.py:142
  65.6 0.9 broadcast_in_dim.2
  66.5 3.5 %all-to-all-start.1 = ((bf16[8,2,16,1024]{3,2,1,0:T(8,128)(2,1)}), bf16[8,2,16,1024]{3,2,1,0:T(8,128)(2,1)S(1)}, u32[]{:S(2)}, u32[]{:S(2)}) async-start(bf16[8,2,16,1024]{3,2,1,0:T(8,128)(2,1)} %broadcast_in_dim.2), calls=%async_computation.2 | async-start | bytes 1048576 | tf_op jit(solution)/shard_map/all_to_all | solution.py:133
  70.0 0.9 fusion.34
  70.9 0.8 collective-permute-start.2
  71.7 0.7 collective-permute-start.1
  72.4 0.7 collective-permute-start
  73.1 1.3 %maximum_select_fusion = bf16[2,512,512]{2,1,0:T(8,128)(2,1)S(1)} fusion(bf16[2,512,512]{2,1,0:T(8,128)(2,1)S(1)} %copy-done, bf16[2,512,256]{2,1,0:T(8,128)(2,1)} %get-tuple-element.22, bf16[2,512,256]{2,1,0:T(8,128)(2,1)S(1)} %get-tuple-element.21, pred[]{:T(512)S(6)} %eq.12), kind=kLoop, calls=%fused_computation.24 | loop fusion | flops 2621440 | bytes 3145729 | tf_op jit(solution)/shard_map/jit(_where)/select_n | solution.py:196
  74.4 0.1 add_select_fusion
  74.5 0.7 collective-permute-start.5
  75.2 0.7 collective-permute-start.4
  75.8 1.3 %collective-permute-start.3 = (bf16[128,1024]{1,0:T(8,128)(2,1)S(1)}, bf16[128,1024]{1,0:T(8,128)(2,1)}, u32[]{:S(2)}, u32[]{:S(2)}) collective-permute-start(bf16[128,1024]{1,0:T(8,128)(2,1)S(1)} %add_select_fusion), channel_id=1, source_target_pairs={{0,9},{8,11},{2,4},{6,12},{16,25},{24,27},{18,20},{22,28},{32,41},... | collective-permute-start | bytes 786440 | tf_op jit(solution)/shard_map/ppermute | solution.py:154
  77.1 7.7 %all-to-all-done.1 = bf16[8,2,16,1024]{3,2,1,0:T(8,128)(2,1)S(1)} async-done(((bf16[8,2,16,1024]{3,2,1,0:T(8,128)(2,1)}), bf16[8,2,16,1024]{3,2,1,0:T(8,128)(2,1)S(1)}, u32[]{:S(2)}, u32[]{:S(2)}) %all-to-all-start.1) | async-done | bytes 524320 | tf_op jit(solution)/shard_map/all_to_all | solution.py:133
  84.8 1.9 %collective-permute-start.9 = (bf16[256,1024]{1,0:T(8,128)(2,1)S(1)}, bf16[256,1024]{1,0:T(8,128)(2,1)S(1)}, u32[]{:S(2)}, u32[]{:S(2)}) collective-permute-start(bf16[256,1024]{1,0:T(8,128)(2,1)S(1)} %bitcast.35), channel_id=1, source_target_pairs={{0,16},{16,0},{32,48},{48,32},{1,17},{17,1},{33,49},{49,33},{2,18}... | collective-permute-start | bytes 1572872 | tf_op jit(solution)/shard_map/ppermute | solution.py:142
  86.7 0.1 slice_bitcast_fusion.1
  86.9 8.1 %collective-permute-done.3 = bf16[128,1024]{1,0:T(8,128)(2,1)} collective-permute-done((bf16[128,1024]{1,0:T(8,128)(2,1)S(1)}, bf16[128,1024]{1,0:T(8,128)(2,1)}, u32[]{:S(2)}, u32[]{:S(2)}) %collective-permute-start.3) | collective-permute-done | bytes 262176 | tf_op jit(solution)/shard_map/ppermute | solution.py:154
  95.0 1.0 add_add_fusion
  96.0 0.1 slice_negate_fusion.2
  96.1 1.3 %reduce-precision_convert_fusion = (bf16[512,1024]{1,0:T(8,128)(2,1)S(1)}, bf16[512,1024]{1,0:T(8,128)(2,1)S(1)}) fusion(bf16[512,512]{1,0:T(8,128)(2,1)S(1)} %get-tuple-element.24, bf16[512,512]{1,0:T(8,128)(2,1)S(1)} %get-tuple-element.23, bf16[256,1024]{1,0:T(8,128)(2,1)S(1)} %collective-permute-done.9, bf16[256,1024]{1,0:T(8,128)(2,1)S(1)} %bitcast.37, ...), kind=kOutput, calls=%fused_computation.13 | convolution fusion | flops 1086324736 | bytes 5242880 | tf_op jit(solution)/shard_map/dot_general | solution.py:137
  97.4 0.1 slice_negate_fusion
  97.6 0.8 copy-done.2
  98.4 0.8 fusion.21
  99.2 0.8 maximum_bitcast_fusion
  (19 shorter events, 0.2 us)
Async XLA Ops:
  6.5 64.3 %reduce-scatter.2.cloned.1.call-start = ((), (), s32[]{:S(2)}) async-start(), calls=%async_computation.3 | async-start | bytes 2359296 | tf_op jit(solution)/shard_map/reduce_scatter | solution.py:177
  15.2 54.8 %copy-start = (bf16[2,512,512]{2,1,0:T(8,128)(2,1)S(1)}, bf16[2,512,512]{2,1,0:T(8,128)(2,1)}, u32[]{:S(2)}) copy-start(bf16[2,512,512]{2,1,0:T(8,128)(2,1)} %param.13) | copy-start | bytes 3145732
  15.2 4.1 %collective-permute-start.6 = (bf16[256,1024]{1,0:T(8,128)(2,1)}, bf16[256,1024]{1,0:T(8,128)(2,1)S(1)}, u32[]{:S(2)}, u32[]{:S(2)}) collective-permute-start(bf16[256,1024]{1,0:T(8,128)(2,1)} %get-tuple-element.11), channel_id=1, source_target_pairs={{0,16},{16,0},{32,48},{48,32},{1,17},{17,1},{33,49},{49,33},{2,18}... | collective-permute-start | bytes 1572872 | tf_op jit(solution)/shard_map/ppermute | solution.py:142
  20.4 11.7 %collective-permute-start.7 = (bf16[8,16,1024]{2,1,0:T(8,128)(2,1)S(1)}, bf16[8,16,1024]{2,1,0:T(8,128)(2,1)S(1)}, u32[]{:S(2)}, u32[]{:S(2)}) collective-permute-start(bf16[8,16,1024]{2,1,0:T(8,128)(2,1)S(1)} %add_bitcast_fusion), channel_id=1, source_target_pairs={{0,32},{16,48},{32,0},{48,16},{1,33},{17,49},{33,1},{49,17},{2,34}... | collective-permute-start | bytes 786440 | tf_op jit(solution)/shard_map/ppermute | solution.py:142
  58.3 7.3 %collective-permute-start.8 = (bf16[16,1024]{1,0:T(8,128)(2,1)S(1)}, bf16[16,1024]{1,0:T(8,128)(2,1)S(1)}, u32[]{:S(2)}, u32[]{:S(2)}) collective-permute-start(bf16[16,1024]{1,0:T(8,128)(2,1)S(1)} %reduce_sum.12), channel_id=1, source_target_pairs={{0,32},{16,48},{32,0},{48,16},{1,33},{17,49},{33,1},{49,17},{2,34}... | collective-permute-start | bytes 98312 | tf_op jit(solution)/shard_map/ppermute | solution.py:142
  66.5 18.3 %all-to-all-start.1 = ((bf16[8,2,16,1024]{3,2,1,0:T(8,128)(2,1)}), bf16[8,2,16,1024]{3,2,1,0:T(8,128)(2,1)S(1)}, u32[]{:S(2)}, u32[]{:S(2)}) async-start(bf16[8,2,16,1024]{3,2,1,0:T(8,128)(2,1)} %broadcast_in_dim.2), calls=%async_computation.2 | async-start | bytes 1048576 | tf_op jit(solution)/shard_map/all_to_all | solution.py:133
  70.9 3.5 %copy-start.1 = (bf16[128,1024]{1,0:T(8,128)(2,1)S(1)}, bf16[128,1024]{1,0:T(8,128)(2,1)}, u32[]{:S(2)}) copy-start(bf16[128,1024]{1,0:T(8,128)(2,1)} %reduce-scatter.2.cloned.1.call-done) | copy-start | bytes 786436
  70.9 3.5 %collective-permute-start.2 = (bf16[128,1024]{1,0:T(8,128)(2,1)}, bf16[128,1024]{1,0:T(8,128)(2,1)S(1)}, u32[]{:S(2)}, u32[]{:S(2)}) collective-permute-start(bf16[128,1024]{1,0:T(8,128)(2,1)} %reduce-scatter.2.cloned.1.call-done), channel_id=1, source_target_pairs={{0,6},{16,22},{32,38},{48,54},{64,70},{80,86},{96,102},{112,118},{... | collective-permute-start | bytes 786440 | tf_op jit(solution)/shard_map/ppermute | solution.py:188
  71.7 2.7 %collective-permute-start.1 = (bf16[128,1024]{1,0:T(8,128)(2,1)}, bf16[128,1024]{1,0:T(8,128)(2,1)S(1)}, u32[]{:S(2)}, u32[]{:S(2)}) collective-permute-start(bf16[128,1024]{1,0:T(8,128)(2,1)} %reduce-scatter.2.cloned.1.call-done), channel_id=1, source_target_pairs={{0,2},{16,18},{32,34},{48,50},{64,66},{80,82},{96,98},{112,114},{1... | collective-permute-start | bytes 786440 | tf_op jit(solution)/shard_map/ppermute | solution.py:188
  72.4 2.0 %collective-permute-start = (bf16[128,1024]{1,0:T(8,128)(2,1)}, bf16[128,1024]{1,0:T(8,128)(2,1)S(1)}, u32[]{:S(2)}, u32[]{:S(2)}) collective-permute-start(bf16[128,1024]{1,0:T(8,128)(2,1)} %reduce-scatter.2.cloned.1.call-done), channel_id=1, source_target_pairs={{0,8},{16,24},{32,40},{48,56},{64,72},{80,88},{96,104},{112,120},{... | collective-permute-start | bytes 786440 | tf_op jit(solution)/shard_map/ppermute | solution.py:188
  74.5 12.4 %collective-permute-start.5 = (bf16[128,1024]{1,0:T(8,128)(2,1)S(1)}, bf16[128,1024]{1,0:T(8,128)(2,1)S(1)}, u32[]{:S(2)}, u32[]{:S(2)}) collective-permute-start(bf16[128,1024]{1,0:T(8,128)(2,1)S(1)} %add_select_fusion), channel_id=1, source_target_pairs={{0,1},{8,15},{2,3},{6,5},{16,17},{24,31},{18,19},{22,21},{32,33},{... | collective-permute-start | bytes 786440 | tf_op jit(solution)/shard_map/ppermute | solution.py:154
  75.2 11.7 %collective-permute-start.4 = (bf16[128,1024]{1,0:T(8,128)(2,1)S(1)}, bf16[128,1024]{1,0:T(8,128)(2,1)S(1)}, u32[]{:S(2)}, u32[]{:S(2)}) collective-permute-start(bf16[128,1024]{1,0:T(8,128)(2,1)S(1)} %add_select_fusion), channel_id=1, source_target_pairs={{0,7},{8,13},{2,10},{6,14},{16,23},{24,29},{18,26},{22,30},{32,39}... | collective-permute-start | bytes 786440 | tf_op jit(solution)/shard_map/ppermute | solution.py:154
  75.8 19.1 %collective-permute-start.3 = (bf16[128,1024]{1,0:T(8,128)(2,1)S(1)}, bf16[128,1024]{1,0:T(8,128)(2,1)}, u32[]{:S(2)}, u32[]{:S(2)}) collective-permute-start(bf16[128,1024]{1,0:T(8,128)(2,1)S(1)} %add_select_fusion), channel_id=1, source_target_pairs={{0,9},{8,11},{2,4},{6,12},{16,25},{24,27},{18,20},{22,28},{32,41},... | collective-permute-start | bytes 786440 | tf_op jit(solution)/shard_map/ppermute | solution.py:154
  84.8 11.2 %collective-permute-start.9 = (bf16[256,1024]{1,0:T(8,128)(2,1)S(1)}, bf16[256,1024]{1,0:T(8,128)(2,1)S(1)}, u32[]{:S(2)}, u32[]{:S(2)}) collective-permute-start(bf16[256,1024]{1,0:T(8,128)(2,1)S(1)} %bitcast.35), channel_id=1, source_target_pairs={{0,16},{16,0},{32,48},{48,32},{1,17},{17,1},{33,49},{49,33},{2,18}... | collective-permute-start | bytes 1572872 | tf_op jit(solution)/shard_map/ppermute | solution.py:142
  97.4 1.0 copy-start.2
Sparse Core Ops, SparseCore 0:
  15.3 53.8 reduce-scatter.1
